TPU v7x, 32 devices: a whole 2x2x4 slice. The times are simulated.
32 devices in a mesh: src: 16 (over z, y, x), lev: 2 (over core).
Axes of the slice: x: 2, y: 2, z: 4, core: 2. Of those that a mesh axis runs over, the one named last changes fastest.
Arguments:
- field: bfloat16 [32768, 256], P('src', 'lev'), may hold values from -6 to 6
- grad_coef: float32 [2, 4, 32768], P(None, None, 'src'), may hold values from -6 to 6
- neighbours: int32 [32768, 4], P('src'), may hold values from 0 to 2175, as said below
- level_weight: float32 [8], replicated, may hold values from 0.2 to 2
- src_index: int32 [2048, 64], P('src'), may hold values from 0 to 2047
- tgt_index: int32 [2048, 32], P('src'), may hold values from 0 to 1023
- block_dest: int32 [2048, 1], P('src'), may hold values from 0 to 15; in each aligned block of 128 rows (0 to 127, 128 to 255, ...) at most 16 rows name the same one
- weights: bfloat16 [2048, 6144], P('src'), may hold values from -0.21875 to 0.21875
Outputs:
- remapped: bfloat16 [16384, 256], P('src', 'lev')
- column_total: float32 [32, 16384], P(None, 'src')
Inputs may be any that keep to these rules, and one draw needn't show every extreme that they name: `neighbours`: position 64 + p is the device's own cell p; positions below 64 and from 2112 on are the last and first cells of the devices before and after along the closed curve; a neighbour lies at most 64 cells from the cell. `block_dest`: the 128 blocks of one index of src name one target index at most 16 times.
All inputs are finite; a program needn't handle non-finite values.
Results may differ from a plain program's by a relative error of at most 0.0049.
Values may be sent and summed in bfloat16 or wider, within the bound.
A program may use at most 128 MiB of HBM per device.

v0:
```python
import jax
import jax.numpy as jnp
from jax import lax
from jax.sharding import PartitionSpec as P

FIELDS = 32
HW = 64
SB = 64
TB = 32
T_DEV = 1024


def extended_2(block, sides, width):
    for axis, dim in sides:
        count = lax.axis_size(axis)
        forward = [(i, i + 1) for i in range(count - 1)]
        forward.append((count - 1, 0))
        backward = [(target, source) for source, target in forward]
        low = lax.ppermute(
            lax.slice_in_dim(block, block.shape[dim] - width, None, axis=dim), axis, forward
        )
        high = lax.ppermute(lax.slice_in_dim(block, 0, width, axis=dim), axis, backward)
        block = jnp.concatenate([low, block, high], axis=dim)
    return block


def block_product(block_weights, block_rows):
    block_count = block_rows.shape[0]
    shaped = block_weights.reshape(block_count, 3 * SB, TB)
    return lax.dot_general(
        shaped, block_rows, (((1,), (1,)), ((0,), (0,))), preferred_element_type=jnp.float32
    )


def shards(field, grad_coef, neighbours, level_weight, src_index, tgt_index, block_dest, weights):
    extended = extended_2(field, (("src", 0),), HW)
    own_float = field.astype(jnp.float32)
    differ = extended[neighbours].astype(jnp.float32) - own_float[:, None, :]
    grad_east = jnp.sum(grad_coef[0].T[:, :, None] * differ, axis=1).astype(jnp.bfloat16)
    grad_north = jnp.sum(grad_coef[1].T[:, :, None] * differ, axis=1).astype(jnp.bfloat16)
    recon = jnp.stack([field, grad_east, grad_north])
    columns = field.shape[1]
    block_count = src_index.shape[0]
    block_rows = jnp.transpose(recon[:, src_index], (1, 0, 2, 3)).reshape(
        block_count, 3 * SB, columns
    )
    src_count = lax.axis_size("src")
    capacity = 2 * block_count // src_count
    target_owner = block_dest[:, 0]
    onehot = (target_owner[:, None] == jnp.arange(src_count, dtype=jnp.int32)[None, :]).astype(
        jnp.int32
    )
    before = jnp.cumsum(onehot, axis=0) - onehot
    slot_rank = jnp.sum(before * onehot, axis=1)
    slot_index = target_owner * capacity + slot_rank
    slots = src_count * capacity
    send_cells = jnp.zeros((slots, TB), jnp.int32).at[slot_index].set(tgt_index)
    recv_cells = lax.all_to_all(send_cells, "src", split_axis=0, concat_axis=0, tiled=True)
    partial_value = block_product(weights, block_rows)
    send_partial = jnp.zeros((slots, TB, columns), jnp.float32).at[slot_index].set(partial_value)
    received = lax.all_to_all(send_partial, "src", split_axis=0, concat_axis=0, tiled=True)
    total = (
        jnp.zeros((T_DEV, columns), jnp.float32)
        .at[recv_cells.reshape(-1)]
        .add(received.reshape(-1, columns))
    )
    remapped = total.astype(jnp.bfloat16)
    level_count = columns // FIELDS
    level_share = lax.dynamic_slice_in_dim(
        level_weight, lax.axis_index("lev") * level_count, level_count
    )
    local_sum = jnp.einsum(
        "tlf,l->ft",
        total.reshape(T_DEV, level_count, FIELDS),
        level_share,
        precision=lax.Precision.HIGHEST,
    )
    column_total = lax.psum(local_sum, "lev")
    return (remapped, column_total)


def solution(mesh):
    placed = (
        P("src", "lev"),
        P(None, None, "src"),
        P("src", None),
        P(),
        P("src", None),
        P("src", None),
        P("src", None),
        P("src", None),
    )
    return jax.shard_map(
        shards,
        mesh=mesh,
        in_specs=placed,
        out_specs=(P("src", "lev"), P(None, "src")),
        check_vma=False,
    )
```

profile of v0, /device:TPU:15, one launch (start us, length us, event | category | flops | bytes accessed | tf_op | source)
XLA Modules:
  0.0 407.3 jit_solution(9051789890176872774)
XLA Ops:
  7.2 0.8 fusion.14
  8.0 1.2 collective-permute-start
  10.4 0.8 select_reduce_fusion
  11.9 0.8 copy.23
  12.7 0.9 scatter_custom_fusion
  14.3 7.2 %all-to-all-start = ((s32[16,1,512]{2,1,0:T(1,128)}), s32[16,1,512]{2,1,0:T(1,128)S(1)}, u32[]{:S(2)}, u32[]{:S(2)}) async-start(s32[16,1,512]{2,1,0:T(1,128)} %reshape.126), calls=%async_computation | async-start | bytes 65536 | tf_op jit(solution)/shard_map/all_to_all | solution.py:58
  21.5 0.8 compare_select_fusion.2
  23.3 0.8 slice_bitcast_fusion
  24.1 0.8 compare_select_fusion.1
  25.0 2.1 convert_element_type.40
  27.1 1.4 copy.24
  28.5 1.4 copy.26
  29.9 8.9 %copy.27 = bf16[1,2048,128]{2,0,1:T(2,128)(2,1)} copy(bf16[1,2048,128]{2,1,0:T(8,128)(2,1)S(1)} %bitcast.47) | data formatting | bytes 1048576 | tf_op jit(solution)/shard_map/stack | solution.py:41
  38.8 1.9 copy.32
  40.7 3.4 copy.33
  44.1 24.0 %gather_fusion = bf16[8192,128]{1,0:T(8,128)(2,1)S(1)} fusion(bf16[2176,128]{1,0:T(8,128)(2,1)S(1)} %pad_maximum_fusion.1, s32[8192]{0:T(1024)S(1)} %broadcast_clamp_fusion.1), kind=kCustom, calls=%fused_computation | custom fusion | bytes 4227072 | tf_op jit(solution)/shard_map/gather | solution.py:38
  68.2 15.1 %fusion.2 = (bf16[2048,128]{1,0:T(8,128)(2,1)S(1)}, bf16[2048,128]{1,0:T(8,128)(2,1)S(1)}) fusion(bf16[2048,4,128]{2,1,0:T(4,128)(2,1)S(1)} %bitcast.45, f32[2048,128]{1,0:T(8,128)} %convert_element_type.40, f32[2048,4]{1,0:T(8,128)} %copy.24, f32[2048,4]{1,0:T(8,128)} %copy.26), kind=kLoop, calls=%fused_computation.8 | loop fusion | flops 5767168 | bytes 4259840 | tf_op jit(solution)/shard_map/reduce_sum | solution.py:39
  83.2 8.3 %copy.28 = bf16[1,2048,128]{2,0,1:T(2,128)(2,1)S(1)} copy(bf16[1,2048,128]{2,1,0:T(8,128)(2,1)S(1)} %bitcast.50) | data formatting | bytes 1048576 | tf_op jit(solution)/shard_map/convert_element_type | solution.py:39
  91.6 8.1 %copy.29 = bf16[1,2048,128]{2,0,1:T(2,128)(2,1)S(1)} copy(bf16[1,2048,128]{2,1,0:T(8,128)(2,1)S(1)} %bitcast.49) | data formatting | bytes 1048576 | tf_op jit(solution)/shard_map/convert_element_type | solution.py:40
  99.7 3.6 pad_maximum_fusion
  103.3 56.5 %gather_fusion.1 = bf16[8192,3,128]{2,1,0:T(4,128)(2,1)} fusion(bf16[3,2048,128]{2,0,1:T(4,128)(2,1)S(1)} %pad_maximum_fusion, s32[8192]{0:T(1024)S(1)} %broadcast_clamp_fusion), kind=kCustom, calls=%fused_computation.1 | custom fusion | bytes 12615680 | tf_op jit(solution)/shard_map/gather | solution.py:44
  159.7 5.5 %copy.31 = bf16[128,3,64,128]{3,2,1,0:T(8,128)(2,1)S(1)} copy(bf16[128,3,64,128]{3,1,2,0:T(4,128)(2,1)} %bitcast.43) | data formatting | bytes 12582912 | tf_op jit(solution)/shard_map/transpose | solution.py:44
  165.2 2.4 convolution_bitcast_fusion
  167.7 2.5 broadcast_in_dim.24
  170.2 15.7 %scatter_fusion = f32[256,32,128]{2,1,0:T(8,128)} fusion(f32[256,32,128]{2,1,0:T(8,128)} %broadcast_in_dim.24, s32[128]{0:T(128)S(1)} %fusion.11, f32[128,32,128]{2,1,0:T(8,128)S(1)} %convolution_bitcast_fusion), kind=kCustom, calls=%fused_computation.3 | custom fusion | bytes 6291968 | tf_op jit(solution)/shard_map/scatter | solution.py:60
  185.9 6.4 %all-to-all-start.1 = ((f32[256,32,128]{2,1,0:T(8,128)}), f32[256,32,128]{2,1,0:T(8,128)}, u32[]{:S(2)}, u32[]{:S(2)}) async-start(f32[256,32,128]{2,1,0:T(8,128)} %scatter_fusion), calls=%async_computation.1 | async-start | bytes 8388608 | tf_op jit(solution)/shard_map/all_to_all | solution.py:61
  193.9 92.0 %all-to-all-done.1 = f32[256,32,128]{2,1,0:T(8,128)} async-done(((f32[256,32,128]{2,1,0:T(8,128)}), f32[256,32,128]{2,1,0:T(8,128)}, u32[]{:S(2)}, u32[]{:S(2)}) %all-to-all-start.1) | async-done | bytes 4194336 | tf_op jit(solution)/shard_map/all_to_all | solution.py:61
  285.9 44.4 %scatter_custom_fusion.2 = f32[1024,128]{1,0:T(8,128)S(1)} fusion(s32[8192]{0:T(1024)S(1)} %bitcast.53, f32[8192,128]{1,0:T(8,128)} %bitcast.18, f32[]{:T(128)} %constant.10.clone.1), kind=kCustom, calls=%fused_computation.17 | custom fusion | flops 1048576 | bytes 524800 | tf_op jit(solution)/shard_map/scatter-add | solution.py:65
  330.5 29.1 %fusion.4 = f32[1,1024,32]{0,1,2:T(8,128)} fusion(f32[1024,4,32]{0,2,1:T(8,128)S(1)} %bitcast.48, f32[8]{0:T(128)S(1)} %copy-done, s32[]{:T(128)S(6)} %select_n.28), kind=kOutput, calls=%fused_computation.13 | convolution fusion | flops 1572864 | bytes 655396 | tf_op jit(solution)/shard_map/tlf,l->ft/dot_general | solution.py:72
  359.7 10.6 %copy.36 = f32[1,1024,32]{1,2,0:T(8,128)} copy(f32[1,1024,32]{0,1,2:T(8,128)} %fusion.4) | data formatting | bytes 262144 | tf_op jit(solution)/shard_map/tlf,l->ft/dot_general | solution.py:72
  371.0 27.8 %all-reduce.2.cloned.1.call-done = f32[32,1024]{1,0:T(8,128)} async-done(((f32[32,1024]{1,0:T(8,128)}), f32[32,1024]{1,0:T(8,128)}) %all-reduce.2.cloned.1.call-update) | async-done | bytes 131088 | tf_op jit(solution)/shard_map/psum | solution.py:78
  398.9 1.6 copy.41
  (32 shorter events, 6.3 us)
Async XLA Ops:
  7.2 323.4 %copy-start = (f32[8]{0:T(128)S(1)}, f32[8]{0:T(128)}, u32[]{:S(2)}) copy-start(f32[8]{0:T(128)} %param.11) | copy-start | bytes 100
  7.2 22.7 %copy-start.2 = (bf16[2048,128]{1,0:T(8,128)(2,1)S(1)}, bf16[2048,128]{1,0:T(8,128)(2,1)}, u32[]{:S(2)}) copy-start(bf16[2048,128]{1,0:T(8,128)(2,1)} %param.8) | copy-start | bytes 1572868
  8.0 36.1 %collective-permute-start = (bf16[64,128]{1,0:T(8,128)(2,1)S(1)}, bf16[64,128]{1,0:T(8,128)(2,1)S(1)}, u32[]{:S(2)}, u32[]{:S(2)}) collective-permute-start(bf16[64,128]{1,0:T(8,128)(2,1)S(1)} %get-tuple-element.4), channel_id=1, source_target_pairs={{0,2},{2,4},{4,6},{6,8},{8,10},{10,12},{12,14},{14,16},{16,18},{18... | collective-permute-start | bytes 49160 | tf_op jit(solution)/shard_map/ppermute | solution.py:19
  9.2 34.9 %collective-permute-start.1 = (bf16[64,128]{1,0:T(8,128)(2,1)S(1)}, bf16[64,128]{1,0:T(8,128)(2,1)S(1)}, u32[]{:S(2)}, u32[]{:S(2)}) collective-permute-start(bf16[64,128]{1,0:T(8,128)(2,1)S(1)} %get-tuple-element.5), channel_id=1, source_target_pairs={{2,0},{4,2},{6,4},{8,6},{10,8},{12,10},{14,12},{16,14},{18,16},{20... | collective-permute-start | bytes 49160 | tf_op jit(solution)/shard_map/ppermute | solution.py:22
  14.3 171.5 %all-to-all-start = ((s32[16,1,512]{2,1,0:T(1,128)}), s32[16,1,512]{2,1,0:T(1,128)S(1)}, u32[]{:S(2)}, u32[]{:S(2)}) async-start(s32[16,1,512]{2,1,0:T(1,128)} %reshape.126), calls=%async_computation | async-start | bytes 65536 | tf_op jit(solution)/shard_map/all_to_all | solution.py:58
  68.2 31.5 %copy-start.3 = (bf16[1,2048,128]{2,0,1:T(2,128)(2,1)S(1)}, bf16[1,2048,128]{2,0,1:T(2,128)(2,1)}, u32[]{:S(2)}) copy-start(bf16[1,2048,128]{2,0,1:T(2,128)(2,1)} %copy.27) | copy-start | bytes 1572868
  159.7 5.5 %copy-start.1 = (bf16[128,192,32]{1,2,0:T(8,128)(2,1)S(1)}, bf16[128,192,32]{1,2,0:T(8,128)(2,1)}, u32[]{:S(2)}) copy-start(bf16[128,192,32]{1,2,0:T(8,128)(2,1)} %copy.33) | copy-start | bytes 4718596
  185.9 100.0 %all-to-all-start.1 = ((f32[256,32,128]{2,1,0:T(8,128)}), f32[256,32,128]{2,1,0:T(8,128)}, u32[]{:S(2)}, u32[]{:S(2)}) async-start(f32[256,32,128]{2,1,0:T(8,128)} %scatter_fusion), calls=%async_computation.1 | async-start | bytes 8388608 | tf_op jit(solution)/shard_map/all_to_all | solution.py:61
  192.3 206.5 %all-reduce.2.cloned.1.call-start = ((), (), s32[]{:S(2)}) async-start(), calls=%async_computation.2 | async-start | bytes 262144 | tf_op jit(solution)/shard_map/psum | solution.py:78
Sparse Core Ops, SparseCore 0:
  370.4 28.4 all-reduce.1
where the time goes:
time: 408 us; the launch traced here: 407 us
  local copies, waits for them, and re-layouts  156 us (38%)
  waiting for transfers between devices  120 us (29%)
  other arithmetic  70.6 us (17%)
  matrix products  31.6 us (8%)
  starting transfers between devices  15.1 us (4%)
  between operations  14.2 us (3%)
    all_to_all x1, waiting for transfers between devices, shards(): lax.all_to_all(send_partial, 'src', split_axis=0, concat_axis=0, tiled=True)  92 us
    gather x1, local copies, waits for them, and re-layouts, shards(): recon[:, src_index]  56.5 us
    scatter-add x1, other arithmetic, shards(): total = jnp.zeros((T_DEV, columns), jnp.float32).at[recv_cells.reshape(-1...  44.4 us
    dot_general x1, matrix products, shards(): jnp.einsum('tlf,l->ft', total.reshape(T_DEV, level_count, FIELDS), level_...  29.1 us
    psum x1, waiting for transfers between devices, shards(): column_total = lax.psum(local_sum, 'lev')  27.8 us
    gather x1, local copies, waits for them, and re-layouts, shards(): differ = extended[neighbours].astype(jnp.float32) - own_float[:, None, :]  24 us
    scatter x1, local copies, waits for them, and re-layouts, shards(): jnp.zeros((slots, TB, columns), jnp.float32).at[slot_index]  15.7 us
    reduce_sum x1, other arithmetic, shards(): jnp.sum(grad_coef[0].T[:, :, None] * differ, axis=1).astype(jnp.bfloat16)  15.1 us
  transfers between devices with their start and end apart: 5, of which 2 were waited for; matrix products, arithmetic and copies ran while one was open for 42% of the time, Pallas kernels for 0%

commit v1 on v0

v1 whole, which is shorter than its diff:
```python
import functools

import jax
import jax.numpy as jnp
from jax import lax
from jax.experimental import pallas as pl
from jax.experimental.pallas import tpu as pltpu
from jax.sharding import PartitionSpec as P

FIELDS = 32
HW = 64
SB = 64
TB = 32
T_DEV = 1024
LANES = 128
SUB = 8
TILE = 128
GROUP = LANES // TB
CHUNKS = ((0.0, 1.0),)


def contract_first(a, b):
    return lax.dot_general(a, b, (((0,), (0,)), ((), ())), preferred_element_type=jnp.float32)


def partial_kernel(
    first, last, src_count,
    src_ref, dest_ref, low_ref, field_ref, high_ref, coef_ref, near_ref, tgt_ref, weight_ref,
    send_ref, cells_ref,
    ext, recon, picked, count, block_list, slot_list,
):
    cells, columns = field_ref.shape
    blocks = tgt_ref.shape[0]
    ranks = last - first
    window = TILE + 2 * HW

    send_ref[...] = jnp.zeros_like(send_ref)
    cells_ref[...] = jnp.zeros_like(cells_ref)

    ext[0:HW, :] = low_ref[...]
    ext[HW:HW + cells, :] = field_ref[...]
    ext[HW + cells:HW + cells + HW, :] = high_ref[...]

    @pl.loop(0, src_count)
    def _(d):
        count[d] = 0

    def place(b, used):
        d = dest_ref[b]
        rank = count[d]
        count[d] = rank + 1
        block_list[used] = b
        slot_list[used] = d * ranks + rank - first
        taken = jnp.logical_and(rank >= first, rank < last)
        return used + taken.astype(jnp.int32)

    used = lax.fori_loop(0, blocks, place, jnp.int32(0))

    @pl.when(used > 0)
    def _():
        block_list[used] = block_list[used - 1]
        slot_list[used] = slot_list[used - 1]

    @pl.loop(0, cells // TILE)
    def _(t):
        base = pl.multiple_of(t * TILE, TILE)
        near = near_ref[:, pl.ds(base, TILE)] - base
        coef = [coef_ref[g, :, pl.ds(base, TILE)] for g in range(2)]
        place_w = lax.broadcasted_iota(jnp.int32, (window, TILE), 0)
        own = place_w == lax.broadcasted_iota(jnp.int32, (window, TILE), 1) + HW
        hits = [place_w == near[k:k + 1, :] for k in range(near.shape[0])]
        held = ext[pl.ds(base, window), :]
        rows = pl.multiple_of(base * SUB, TILE * SUB)
        recon[pl.ds(rows, TILE, stride=SUB), :] = field_ref[pl.ds(base, TILE), :].astype(
            jnp.float32
        )
        for g in range(2):
            total = -jnp.sum(coef[g], axis=0, keepdims=True)
            mix = jnp.where(own, total, 0.0)
            for k, hit in enumerate(hits):
                mix = mix + jnp.where(hit, coef[g][k:k + 1, :], 0.0)
            high = mix.astype(jnp.bfloat16)
            rest = (mix - high.astype(jnp.float32)).astype(jnp.bfloat16)
            value = contract_first(high, held) + contract_first(rest, held)
            recon[pl.ds(rows + 1 + g, TILE, stride=SUB), :] = value

    def one(n, buffer):
        b = block_list[n]
        slot = slot_list[n]
        for j in range(SB):
            at = pl.multiple_of(src_ref[j, b] * SUB, SUB)
            buffer[j * SUB:(j + 1) * SUB, :] = recon[pl.ds(at, SUB), :]
        held = weight_ref[b]
        total = None
        for q in range(GROUP):
            parts = [
                buffer[pl.ds(q * SUB + c, SB // GROUP, stride=GROUP * SUB), :] for c in range(3)
            ]
            rows = jnp.concatenate(parts, axis=0).astype(jnp.bfloat16)
            product = contract_first(held[:, q * TB:(q + 1) * TB], rows)
            total = product if total is None else total + product
        send_ref[slot] = total.astype(jnp.bfloat16)
        cells_ref[pl.ds(slot, 1), :] = tgt_ref[pl.ds(b, 1), :]

    @pl.loop(0, (used + 1) // 2)
    def _(n):
        one(2 * n, picked.at[0])
        one(2 * n + 1, picked.at[1])


def partials(first, last, src_count, src_t, dest, low, field, high, coef, near_t, tgt, weight):
    cells, columns = field.shape
    blocks = tgt.shape[0]
    slots = src_count * (last - first)
    smem = pl.BlockSpec(memory_space=pltpu.SMEM)
    vmem = pl.BlockSpec(memory_space=pltpu.VMEM)
    return pl.pallas_call(
        functools.partial(partial_kernel, first, last, src_count),
        out_shape=(
            jax.ShapeDtypeStruct((slots, TB, columns), jnp.bfloat16),
            jax.ShapeDtypeStruct((slots, TB), jnp.int32),
        ),
        in_specs=[smem, smem] + [vmem] * 7,
        out_specs=(vmem, vmem),
        scratch_shapes=[
            pltpu.VMEM((cells + 2 * HW, columns), jnp.bfloat16),
            pltpu.VMEM((cells * SUB, columns), jnp.float32),
            pltpu.VMEM((2, SB * SUB, columns), jnp.float32),
            pltpu.SMEM((src_count,), jnp.int32),
            pltpu.SMEM((blocks + 1,), jnp.int32),
            pltpu.SMEM((blocks + 1,), jnp.int32),
        ],
        compiler_params=pltpu.CompilerParams(vmem_limit_bytes=40 << 20),
        cost_estimate=pl.CostEstimate(
            flops=8 * blocks * SB * 3 * TB * columns,
            bytes_accessed=60_000_000,
            transcendentals=0,
        ),
        name="partials",
    )(src_t, dest, low, field, high, coef, near_t, tgt, weight)


def combine_kernel(parts, level_count, step, level_ref, *refs):
    index_refs, value_refs = refs[:parts], refs[parts:2 * parts]
    remapped_ref, sum_ref, total = refs[2 * parts:]
    targets, columns = total.shape
    total[...] = jnp.zeros_like(total)
    for index_ref, value_ref in zip(index_refs, value_refs):
        lines = step // LANES

        @pl.loop(0, value_ref.shape[0] // step)
        def _(n, index_ref=index_ref, value_ref=value_ref):
            place = lax.broadcasted_iota(jnp.int32, (targets, LANES), 0)
            hits = [
                jnp.where(place == index_ref[pl.ds(n * lines + m, 1), :], 1.0, 0.0).astype(
                    jnp.bfloat16
                )
                for m in range(lines)
            ]
            value = value_ref[pl.ds(pl.multiple_of(n * step, step), step), :]
            total[...] += jnp.dot(
                jnp.concatenate(hits, axis=1), value, preferred_element_type=jnp.float32
            )

    result = total[...]
    remapped_ref[...] = result.astype(jnp.bfloat16)
    start = lax.axis_index("lev") * level_count
    which = lax.broadcasted_iota(jnp.int32, (FIELDS, columns), 1)
    line = lax.broadcasted_iota(jnp.int32, (FIELDS, columns), 0)
    mix = jnp.zeros((FIELDS, columns), jnp.float32)
    for l in range(level_count):
        mix = jnp.where(which == line + l * FIELDS, level_ref[start + l], mix)
    sum_ref[...] = lax.dot_general(
        mix,
        result,
        (((1,), (1,)), ((), ())),
        precision=lax.Precision.HIGHEST,
        preferred_element_type=jnp.float32,
    )


def combine(level_weight, indices, values, level_count):
    columns = values[0].shape[1]
    smem = pl.BlockSpec(memory_space=pltpu.SMEM)
    vmem = pl.BlockSpec(memory_space=pltpu.VMEM)
    parts = len(values)
    rows = values[0].shape[0]
    step = 512 if all(v.shape[0] % 512 == 0 for v in values) else LANES
    return pl.pallas_call(
        functools.partial(combine_kernel, parts, level_count, step),
        out_shape=(
            jax.ShapeDtypeStruct((T_DEV, columns), jnp.bfloat16),
            jax.ShapeDtypeStruct((FIELDS, T_DEV), jnp.float32),
        ),
        in_specs=[smem] + [vmem] * (2 * parts),
        out_specs=(vmem, vmem),
        scratch_shapes=[pltpu.VMEM((T_DEV, columns), jnp.float32)],
        compiler_params=pltpu.CompilerParams(vmem_limit_bytes=40 << 20),
        name="combine",
    )(level_weight, *indices, *values)


def shards(field, grad_coef, neighbours, level_weight, src_index, tgt_index, block_dest, weights):
    src_count = lax.axis_size("src")
    forward = [(i, (i + 1) % src_count) for i in range(src_count)]
    backward = [(target, source) for source, target in forward]
    low = lax.ppermute(field[-HW:], "src", forward)
    high = lax.ppermute(field[:HW], "src", backward)
    columns = field.shape[1]
    blocks = src_index.shape[0]
    capacity = 2 * blocks // src_count
    shaped = weights.reshape(blocks, 3 * SB * TB // LANES, LANES)
    indices, values = [], []
    for begin, end in CHUNKS:
        first, last = int(begin * capacity), int(end * capacity)
        sent, cells = partials(
            first, last, src_count, src_index.T, block_dest[:, 0], low, field, high, grad_coef,
            neighbours.T, tgt_index, shaped,
        )
        width = (last - first) * TB
        cells = lax.all_to_all(
            cells.reshape(src_count, width), "src", split_axis=0, concat_axis=0, tiled=True
        )
        received = lax.all_to_all(sent, "src", split_axis=0, concat_axis=0, tiled=True)
        indices.append(cells.reshape(src_count * width // LANES, LANES))
        values.append(received.reshape(src_count * width, columns))
    remapped, local_sum = combine(level_weight, indices, values, columns // FIELDS)
    lev_count = lax.axis_size("lev")
    column_total = local_sum
    moving = local_sum
    for _ in range(lev_count - 1):
        moving = lax.ppermute(
            moving, "lev", [(i, (i + 1) % lev_count) for i in range(lev_count)]
        )
        column_total = column_total + moving
    return (remapped, column_total)


def solution(mesh):
    placed = (
        P("src", "lev"),
        P(None, None, "src"),
        P("src", None),
        P(),
        P("src", None),
        P("src", None),
        P("src", None),
        P("src", None),
    )
    return jax.shard_map(
        shards,
        mesh=mesh,
        in_specs=placed,
        out_specs=(P("src", "lev"), P(None, "src")),
        check_vma=False,
    )
```

time: 408 us -> 121 us (0.30)
  the two profiles are of different devices: /device:TPU:15 before, /device:TPU:0 now
where the time goes in v1:
time: 121 us; the launch traced here: 120 us
  blocking collectives  59.4 us (49%)
  Pallas kernels  43 us (36%)
  starting transfers between devices  6.97 us (6%)
  waiting for transfers between devices  6.09 us (5%)
  local copies, waits for them, and re-layouts  3.51 us (3%)
    all_to_all x1, blocking collectives, shards(): lax.all_to_all(sent, 'src', split_axis=0, concat_axis=0, tiled=True)  49.5 us
    pallas_call x1, Pallas kernels, partials(): pl.pallas_call(functools.partial(partial_kernel, first, last, src_count),...  34.5 us
    all_to_all x1, blocking collectives, shards(): lax.all_to_all(cells.reshape(src_count, width), 'src', split_axis=0, conc...  9.98 us
    pallas_call x1, Pallas kernels, combine(): pl.pallas_call(functools.partial(combine_kernel, parts, level_count, step...  8.47 us
    ppermute x1, starting transfers between devices, shards(): high = lax.ppermute(field[:HW], 'src', backward)  6.96 us
    ppermute x1, waiting for transfers between devices, shards(): low = lax.ppermute(field[-HW:], 'src', forward)  4.74 us
    unnamed x14, local copies, waits for them, and re-layouts  2.59 us
  transfers between devices with their start and end apart: 3, of which 2 were waited for; matrix products, arithmetic and copies ran while one was open for 2% of the time, Pallas kernels for 0%

profile of v1, /device:TPU:0, one launch (start us, length us, event | category | flops | bytes accessed | tf_op | source)
XLA Modules:
  0.0 120.4 jit_solution(11910144535133180210)
XLA Ops:
  0.6 0.0 copy-start
  0.6 0.0 copy-start.5
  0.7 0.0 copy-start.3
  0.7 0.0 copy-start.4
  0.7 0.0 copy-start.2
  0.7 0.8 fusion
  1.5 7.0 %collective-permute-start.1 = (bf16[64,128]{1,0:T(8,128)(2,1)S(1)}, bf16[64,128]{1,0:T(8,128)(2,1)S(1)}, u32[]{:S(2)}, u32[]{:S(2)}) collective-permute-start(bf16[64,128]{1,0:T(8,128)(2,1)S(1)} %get-tuple-element.10), channel_id=1, source_target_pairs={{2,0},{4,2},{6,4},{8,6},{10,8},{12,10},{14,12},{16,14},{18,16},{20... | collective-permute-start | bytes 49160 | tf_op jit(solution)/shard_map/ppermute | solution.py:208
  8.4 0.0 collective-permute-start
  8.4 0.8 copy.12.tgt_ref
  9.2 1.8 %copy.14 = bf16[16,8,48,128]{3,2,1,0:T(8,128)(2,1)S(1)} copy(bf16[16,8,48,128]{3,1,2,0:T(8,128)(2,1)} %bitcast.13) | data formatting | bytes 3145728
  11.0 0.0 collective-permute-done.1.high_ref
  11.0 4.7 %collective-permute-done.low_ref = bf16[64,128]{1,0:T(8,128)(2,1)S(1)} collective-permute-done((bf16[64,128]{1,0:T(8,128)(2,1)S(1)}, bf16[64,128]{1,0:T(8,128)(2,1)S(1)}, u32[]{:S(2)}, u32[]{:S(2)}) %collective-permute-start) | collective-permute-done | bytes 16416 | tf_op jit(solution)/shard_map/ppermute | solution.py:207
  15.8 0.0 copy-done
  15.8 0.0 copy-done.5
  15.8 0.0 copy-done.3
  15.8 0.0 copy-done.4
  15.8 0.0 copy-done.2
  15.8 34.5 %partials.1 = (bf16[256,32,128]{2,1,0:T(8,128)(2,1)S(1)}, s32[256,32]{1,0:T(8,128)S(1)}) custom-call(s32[64,128]{1,0:T(8,128)S(1)} %bitcast.10, s32[128]{0:T(128)S(1)} %bitcast.12, bf16[64,128]{1,0:T(8,128)(2,1)S(1)} %collective-permute-done.low_ref, bf16[2048,128]{1,0:T(8,128)(2,1)S(1)} %copy-done, bf16[64,128]{1,0:T(8,128)(2,1)S(1)} %collective-permute-done.1.high_ref, ...), custom_call_target="tpu_custom_call" | custom-call | flops 805306368 | bytes 60000000 | tf_op jit(solution)/shard_map/partials/pallas_call | solution.py:117
  50.3 0.1 all_to_all.12
  50.5 10.0 %all_to_all.15 = s32[16,1,512]{2,1,0:T(1,128)S(1)} all-to-all(s32[16,1,512]{2,1,0:T(1,128)S(1)} %all_to_all.12), channel_id=1, replica_groups=mesh['src'=16,'lev'=2] {'src'}, dimensions={0} | all-to-all | bytes 65536 | tf_op jit(solution)/shard_map/all_to_all | solution.py:221
  60.4 0.0 copy-start.1
  60.4 49.5 %all_to_all.16 = bf16[256,32,128]{2,1,0:T(8,128)(2,1)S(1)} all-to-all(bf16[256,32,128]{2,1,0:T(8,128)(2,1)S(1)} %get-tuple-element.7), channel_id=1, replica_groups=mesh['src'=16,'lev'=2] {'src'}, dimensions={0} | all-to-all | bytes 4194304 | tf_op jit(solution)/shard_map/all_to_all | solution.py:224
  109.9 0.0 copy-done.1
  109.9 8.5 %combine.1 = (bf16[1024,128]{1,0:T(8,128)(2,1)}, f32[32,1024]{1,0:T(8,128)S(1)}) custom-call(f32[8]{0:T(128)S(1)} %copy-done.1, s32[64,128]{1,0:T(8,128)S(1)} %bitcast.9, bf16[8192,128]{1,0:T(8,128)(2,1)S(1)} %bitcast.7), custom_call_target="tpu_custom_call" | custom-call | tf_op jit(solution)/shard_map/combine/pallas_call | solution.py:189
  118.4 0.0 collective-permute-start.2
  118.4 1.3 %collective-permute-done.2 = f32[32,1024]{1,0:T(8,128)S(1)} collective-permute-done((f32[32,1024]{1,0:T(8,128)S(1)}, f32[32,1024]{1,0:T(8,128)S(1)}, u32[]{:S(2)}, u32[]{:S(2)}) %collective-permute-start.2) | collective-permute-done | bytes 131104 | tf_op jit(solution)/shard_map/ppermute | solution.py:232
  119.7 0.7 add.3
Async XLA Ops:
  0.6 15.1 %copy-start = (bf16[2048,128]{1,0:T(8,128)(2,1)S(1)}, bf16[2048,128]{1,0:T(8,128)(2,1)}, u32[]{:S(2)}) copy-start(bf16[2048,128]{1,0:T(8,128)(2,1)} %field_ref.1) | copy-start | bytes 1572868
  0.6 15.1 %copy-start.5 = (s32[128,1]{0,1:T(1,128)S(1)}, s32[128,1]{0,1:T(1,128)}, u32[]{:S(2)}) copy-start(s32[128,1]{0,1:T(1,128)} %param.14) | copy-start | bytes 1540
  0.7 15.1 %copy-start.3 = (s32[128,64]{0,1:T(8,128)S(1)}, s32[128,64]{0,1:T(8,128)}, u32[]{:S(2)}) copy-start(s32[128,64]{0,1:T(8,128)} %param.12) | copy-start | bytes 98308
  0.7 15.1 %copy-start.4 = (s32[2048,4]{0,1:T(4,128)S(1)}, s32[2048,4]{0,1:T(4,128)}, u32[]{:S(2)}) copy-start(s32[2048,4]{0,1:T(4,128)} %param.10) | copy-start | bytes 98308
  0.7 15.1 %copy-start.2 = (f32[2,4,2048]{2,1,0:T(4,128)S(1)}, f32[2,4,2048]{2,1,0:T(4,128)}, u32[]{:S(2)}) copy-start(f32[2,4,2048]{2,1,0:T(4,128)} %coef_ref.1) | copy-start | bytes 196612
  1.5 9.5 %collective-permute-start.1 = (bf16[64,128]{1,0:T(8,128)(2,1)S(1)}, bf16[64,128]{1,0:T(8,128)(2,1)S(1)}, u32[]{:S(2)}, u32[]{:S(2)}) collective-permute-start(bf16[64,128]{1,0:T(8,128)(2,1)S(1)} %get-tuple-element.10), channel_id=1, source_target_pairs={{2,0},{4,2},{6,4},{8,6},{10,8},{12,10},{14,12},{16,14},{18,16},{20... | collective-permute-start | bytes 49160 | tf_op jit(solution)/shard_map/ppermute | solution.py:208
  8.4 7.3 %collective-permute-start = (bf16[64,128]{1,0:T(8,128)(2,1)S(1)}, bf16[64,128]{1,0:T(8,128)(2,1)S(1)}, u32[]{:S(2)}, u32[]{:S(2)}) collective-permute-start(bf16[64,128]{1,0:T(8,128)(2,1)S(1)} %get-tuple-element.11), channel_id=1, source_target_pairs={{0,2},{2,4},{4,6},{6,8},{8,10},{10,12},{12,14},{14,16},{16,18},{18... | collective-permute-start | bytes 49160 | tf_op jit(solution)/shard_map/ppermute | solution.py:207
  60.4 49.5 %copy-start.1 = (f32[8]{0:T(128)S(1)}, f32[8]{0:T(128)}, u32[]{:S(2)}) copy-start(f32[8]{0:T(128)} %level_ref.1) | copy-start | bytes 100
  118.4 1.3 %collective-permute-start.2 = (f32[32,1024]{1,0:T(8,128)S(1)}, f32[32,1024]{1,0:T(8,128)S(1)}, u32[]{:S(2)}, u32[]{:S(2)}) collective-permute-start(f32[32,1024]{1,0:T(8,128)S(1)} %get-tuple-element.9), channel_id=1, source_target_pairs={{0,1},{1,0},{2,3},{3,2},{4,5},{5,4},{6,7},{7,6},{8,9},{9,8},{10,11... | collective-permute-start | bytes 393224 | tf_op jit(solution)/shard_map/ppermute | solution.py:232

commit v2 on v1

v2 whole, which is shorter than its diff:
```python
import functools

import jax
import jax.numpy as jnp
from jax import lax
from jax.experimental import pallas as pl
from jax.experimental.pallas import tpu as pltpu
from jax.sharding import PartitionSpec as P

FIELDS = 32
HW = 64
SB = 64
TB = 32
T_DEV = 1024
LANES = 128
SUB = 8
TILE = 128
GROUP = LANES // TB
MESH = pl.DeviceIdType.MESH


def contract_first(a, b):
    return lax.dot_general(a, b, (((0,), (0,)), ((), ())), preferred_element_type=jnp.float32)


def partial_kernel(
    capacity, src_count,
    src_ref, dest_ref, low_ref, field_ref, high_ref, coef_ref, near_ref, tgt_ref, weight_ref,
    send_ref,
    ext, recon, picked, tags, count, home,
):
    cells, columns = field_ref.shape
    blocks = tgt_ref.shape[0]
    rows_each = capacity * TB
    lines = tags.shape[0] // src_count
    window = TILE + 2 * HW

    send_ref[...] = jnp.zeros_like(send_ref)
    tags[...] = jnp.zeros_like(tags)

    ext[0:HW, :] = low_ref[...]
    ext[HW:HW + cells, :] = field_ref[...]
    ext[HW + cells:HW + cells + HW, :] = high_ref[...]

    @pl.loop(0, src_count)
    def _(d):
        count[d] = 0

    lane_group = lax.broadcasted_iota(jnp.int32, (1, LANES), 1) // TB

    @pl.loop(0, blocks)
    def _(b):
        d = dest_ref[b]
        rank = count[d]
        count[d] = rank + 1
        home[b] = d * capacity + rank
        line = pl.ds(d * lines + rank // GROUP, 1)
        tags[line, :] = jnp.where(
            lane_group == rank % GROUP, tgt_ref[pl.ds(b, 1), :], tags[line, :]
        )

    @pl.loop(0, src_count)
    def _(d):
        cell = tags[pl.ds(pl.multiple_of(d * lines, SUB), lines), :]
        digits = jnp.concatenate([cell // 256, cell % 256], axis=0).astype(jnp.float32)
        send_ref[d, rows_each:, :] = digits.astype(jnp.bfloat16)

    @pl.loop(0, cells // TILE)
    def _(t):
        base = pl.multiple_of(t * TILE, TILE)
        near = near_ref[:, pl.ds(base, TILE)] - base
        coef = [coef_ref[g, :, pl.ds(base, TILE)] for g in range(2)]
        place_w = lax.broadcasted_iota(jnp.int32, (window, TILE), 0)
        own = place_w == lax.broadcasted_iota(jnp.int32, (window, TILE), 1) + HW
        hits = [place_w == near[k:k + 1, :] for k in range(near.shape[0])]
        held = ext[pl.ds(base, window), :]
        rows = pl.multiple_of(base * SUB, TILE * SUB)
        recon[pl.ds(rows, TILE, stride=SUB), :] = field_ref[pl.ds(base, TILE), :].astype(
            jnp.float32
        )
        for g in range(2):
            total = -jnp.sum(coef[g], axis=0, keepdims=True)
            mix = jnp.where(own, total, 0.0)
            for k, hit in enumerate(hits):
                mix = mix + jnp.where(hit, coef[g][k:k + 1, :], 0.0)
            high = mix.astype(jnp.bfloat16)
            rest = (mix - high.astype(jnp.float32)).astype(jnp.bfloat16)
            value = contract_first(high, held) + contract_first(rest, held)
            recon[pl.ds(rows + 1 + g, TILE, stride=SUB), :] = value

    def one(b, buffer):
        slot = home[b]
        for j in range(SB):
            at = pl.multiple_of(src_ref[j, b] * SUB, SUB)
            buffer[j * SUB:(j + 1) * SUB, :] = recon[pl.ds(at, SUB), :]
        held = weight_ref[b]
        total = None
        for q in range(GROUP):
            parts = [
                buffer[pl.ds(q * SUB + c, SB // GROUP, stride=GROUP * SUB), :] for c in range(3)
            ]
            rows = jnp.concatenate(parts, axis=0).astype(jnp.bfloat16)
            product = contract_first(held[:, q * TB:(q + 1) * TB], rows)
            total = product if total is None else total + product
        row = pl.multiple_of(slot % capacity * TB, TB)
        send_ref[slot // capacity, pl.ds(row, TB), :] = total.astype(jnp.bfloat16)

    @pl.loop(0, blocks // 2)
    def _(n):
        one(2 * n, picked.at[0])
        one(2 * n + 1, picked.at[1])


def partials(capacity, src_count, src_t, dest, low, field, high, coef, near_t, tgt, weight):
    cells, columns = field.shape
    blocks = tgt.shape[0]
    lines = -(-capacity // (GROUP * SUB)) * SUB
    smem = pl.BlockSpec(memory_space=pltpu.SMEM)
    vmem = pl.BlockSpec(memory_space=pltpu.VMEM)
    return pl.pallas_call(
        functools.partial(partial_kernel, capacity, src_count),
        out_shape=jax.ShapeDtypeStruct(
            (src_count, capacity * TB + 2 * lines, columns), jnp.bfloat16
        ),
        in_specs=[smem, smem] + [vmem] * 7,
        out_specs=vmem,
        scratch_shapes=[
            pltpu.VMEM((cells + 2 * HW, columns), jnp.bfloat16),
            pltpu.VMEM((cells * SUB, columns), jnp.float32),
            pltpu.VMEM((2, SB * SUB, columns), jnp.float32),
            pltpu.VMEM((src_count * lines, LANES), jnp.int32),
            pltpu.SMEM((src_count,), jnp.int32),
            pltpu.SMEM((blocks,), jnp.int32),
        ],
        compiler_params=pltpu.CompilerParams(vmem_limit_bytes=40 << 20),
        cost_estimate=pl.CostEstimate(
            flops=8 * blocks * SB * 3 * TB * columns,
            bytes_accessed=60_000_000,
            transcendentals=0,
        ),
        name="partials",
    )(src_t, dest, low, field, high, coef, near_t, tgt, weight)


def exchange_kernel(
    count, level_count, lev_count, rows, level_ref, send_ref,
    remapped_ref, sum_ref,
    far_in, near_in, total, dense_out, dense_in, local_sum, other_sum,
    out_sem, in_sem, dense_sem, sum_sem,
):
    half = count // 2
    me = lax.axis_index("src")
    lev = lax.axis_index("lev")
    group = (me // half) * half
    place = me - group
    mirror = lax.rem(me + half, count)
    partner = lax.rem(lev + 1, lev_count)
    targets, columns = total.shape
    step = min(LANES, rows)
    lines = rows // step

    def peer(t):
        return group + lax.rem(place + t, half)

    barrier = pltpu.get_barrier_semaphore()

    @pl.loop(1, half)
    def _(t):
        pl.semaphore_signal(barrier, inc=1, device_id=(peer(t), lev), device_id_type=MESH)

    pl.semaphore_signal(barrier, inc=1, device_id=(mirror, lev), device_id_type=MESH)
    pl.semaphore_signal(barrier, inc=1, device_id=(me, partner), device_id_type=MESH)
    pl.semaphore_wait(barrier, half + 1)

    def copy(kind, t):
        to = peer(t)
        owner = lax.rem(to + half, count) if kind == 0 else to
        return pltpu.make_async_remote_copy(
            src_ref=send_ref.at[owner], dst_ref=(far_in, near_in)[kind].at[t],
            send_sem=out_sem.at[kind, t], recv_sem=in_sem.at[kind, t],
            device_id=(to, lev), device_id_type=MESH,
        )

    for kind in range(2):

        @pl.loop(1, half)
        def _(t, kind=kind):
            copy(kind, t).start()

    def add(chunk):
        digits = chunk[rows:, :].astype(jnp.float32)
        lead = digits.shape[0] // 2
        cell = (digits[:lead] * 256.0 + digits[lead:]).astype(jnp.int32)
        where = lax.broadcasted_iota(jnp.int32, (targets, step), 0)
        hits = [
            jnp.where(where == cell[m:m + 1, :step], 1.0, 0.0).astype(jnp.bfloat16)
            for m in range(lines)
        ]
        hits = hits[0] if lines == 1 else jnp.concatenate(hits, axis=1)
        total[...] += jnp.dot(hits, chunk[:rows, :], preferred_element_type=jnp.float32)

    total[...] = jnp.zeros_like(total)
    add(send_ref[mirror])

    @pl.loop(1, half)
    def _(t):
        copy(0, t).wait_recv()
        add(far_in[t])

    dense_out[...] = total[...].astype(jnp.bfloat16)
    dense = pltpu.make_async_remote_copy(
        src_ref=dense_out, dst_ref=dense_in, send_sem=dense_sem.at[0], recv_sem=dense_sem.at[1],
        device_id=(mirror, lev), device_id_type=MESH,
    )
    dense.start()
    total[...] = jnp.zeros_like(total)
    add(send_ref[me])

    @pl.loop(1, half)
    def _(t):
        copy(1, t).wait_recv()
        add(near_in[t])

    dense.wait_recv()
    result = total[...] + dense_in[...].astype(jnp.float32)
    remapped_ref[...] = result.astype(jnp.bfloat16)
    start = lev * level_count
    which = lax.broadcasted_iota(jnp.int32, (FIELDS, columns), 1)
    line = lax.broadcasted_iota(jnp.int32, (FIELDS, columns), 0)
    mix = jnp.zeros((FIELDS, columns), jnp.float32)
    for l in range(level_count):
        mix = jnp.where(which == line + l * FIELDS, level_ref[start + l], mix)
    local_sum[...] = lax.dot_general(
        mix,
        result,
        (((1,), (1,)), ((), ())),
        precision=lax.Precision.HIGHEST,
        preferred_element_type=jnp.float32,
    )
    swap = pltpu.make_async_remote_copy(
        src_ref=local_sum, dst_ref=other_sum, send_sem=sum_sem.at[0], recv_sem=sum_sem.at[1],
        device_id=(me, partner), device_id_type=MESH,
    )
    swap.start()

    @pl.loop(1, half)
    def _(t):
        copy(0, t).wait_send()
        copy(1, t).wait_send()

    dense.wait_send()
    swap.wait()
    sum_ref[...] = local_sum[...] + other_sum[...]


def exchange(level_weight, sent, rows, count, lev_count, level_count):
    columns = sent.shape[2]
    half = count // 2
    smem = pl.BlockSpec(memory_space=pltpu.SMEM)
    vmem = pl.BlockSpec(memory_space=pltpu.VMEM)
    landing = pltpu.VMEM((half,) + sent.shape[1:], jnp.bfloat16)
    return pl.pallas_call(
        functools.partial(exchange_kernel, count, level_count, lev_count, rows),
        out_shape=(
            jax.ShapeDtypeStruct((T_DEV, columns), jnp.bfloat16),
            jax.ShapeDtypeStruct((FIELDS, T_DEV), jnp.float32),
        ),
        in_specs=[smem, vmem],
        out_specs=(vmem, vmem),
        scratch_shapes=[
            landing,
            landing,
            pltpu.VMEM((T_DEV, columns), jnp.float32),
            pltpu.VMEM((T_DEV, columns), jnp.bfloat16),
            pltpu.VMEM((T_DEV, columns), jnp.bfloat16),
            pltpu.VMEM((FIELDS, T_DEV), jnp.float32),
            pltpu.VMEM((FIELDS, T_DEV), jnp.float32),
            pltpu.SemaphoreType.DMA((2, half)),
            pltpu.SemaphoreType.DMA((2, half)),
            pltpu.SemaphoreType.DMA((2,)),
            pltpu.SemaphoreType.DMA((2,)),
        ],
        compiler_params=pltpu.CompilerParams(
            vmem_limit_bytes=40 << 20, collective_id=0, has_side_effects=True
        ),
        name="exchange",
    )(level_weight, sent)


def shards(field, grad_coef, neighbours, level_weight, src_index, tgt_index, block_dest, weights):
    src_count = lax.axis_size("src")
    forward = [(i, (i + 1) % src_count) for i in range(src_count)]
    backward = [(target, source) for source, target in forward]
    low = lax.ppermute(field[-HW:], "src", forward)
    high = lax.ppermute(field[:HW], "src", backward)
    columns = field.shape[1]
    blocks = src_index.shape[0]
    capacity = 2 * blocks // src_count
    shaped = weights.reshape(blocks, 3 * SB * TB // LANES, LANES)
    sent = partials(
        capacity, src_count, src_index.T, block_dest[:, 0], low, field, high, grad_coef,
        neighbours.T, jnp.tile(tgt_index, (1, GROUP)), shaped,
    )
    return exchange(
        level_weight, sent, capacity * TB, src_count, lax.axis_size("lev"), columns // FIELDS
    )


def solution(mesh):
    placed = (
        P("src", "lev"),
        P(None, None, "src"),
        P("src", None),
        P(),
        P("src", None),
        P("src", None),
        P("src", None),
        P("src", None),
    )
    return jax.shard_map(
        shards,
        mesh=mesh,
        in_specs=placed,
        out_specs=(P("src", "lev"), P(None, "src")),
        check_vma=False,
    )
```

time: 121 us -> 88 us (0.73)
  the two profiles are of different devices: /device:TPU:0 before, /device:TPU:15 now
where the time goes in v2:
time: 88 us; the launch traced here: 87.5 us
  Pallas kernels  78.7 us (89%)
  local copies, waits for them, and re-layouts  4.76 us (5%)
  starting transfers between devices  3.26 us (4%)
    pallas_call x1, Pallas kernels, exchange(): pl.pallas_call(functools.partial(exchange_kernel, count, level_count, lev...  43.6 us
    pallas_call x1, Pallas kernels, partials(): pl.pallas_call(functools.partial(partial_kernel, capacity, src_count), ou...  35.1 us
    unnamed x15, local copies, waits for them, and re-layouts  3.21 us
    ppermute x1, starting transfers between devices, shards(): low = lax.ppermute(field[-HW:], 'src', forward)  3.01 us
  transfers between devices with their start and end apart: 2, of which 0 were waited for; matrix products, arithmetic and copies ran while one was open for 3% of the time, Pallas kernels for 0%

profile of v2, /device:TPU:15, one launch (start us, length us, event | category | flops | bytes accessed | tf_op | source)
XLA Modules:
  0.0 87.5 jit_solution(15093586432120837336)
XLA Ops:
  0.6 0.7 fusion
  1.4 0.3 collective-permute-start.1
  1.6 3.0 %collective-permute-start = (bf16[64,128]{1,0:T(8,128)(2,1)S(1)}, bf16[64,128]{1,0:T(8,128)(2,1)S(1)}, u32[]{:S(2)}, u32[]{:S(2)}) collective-permute-start(bf16[64,128]{1,0:T(8,128)(2,1)S(1)} %get-tuple-element.3), channel_id=1, source_target_pairs={{0,2},{2,4},{4,6},{6,8},{8,10},{10,12},{12,14},{14,16},{16,18},{18... | collective-permute-start | bytes 49160 | tf_op jit(solution)/shard_map/ppermute | solution.py:294
  4.6 0.7 tile.4
  5.4 0.1 copy.11.tgt_ref
  5.5 0.0 copy-start
  5.5 0.0 copy-start.1
  5.5 0.0 copy-start.2
  5.5 0.0 copy-start.3
  5.5 0.0 copy-start.4
  5.5 1.8 %copy.12 = bf16[16,8,48,128]{3,2,1,0:T(8,128)(2,1)S(1)} copy(bf16[16,8,48,128]{3,1,2,0:T(8,128)(2,1)} %bitcast.10) | data formatting | bytes 3145728
  7.3 0.0 collective-permute-done.1.high_ref
  7.3 0.0 collective-permute-done.low_ref
  7.3 0.0 copy-done
  7.4 0.0 copy-done.1
  7.4 0.0 copy-done.2
  7.4 0.0 copy-done.3
  7.4 0.0 copy-done.4
  7.4 0.0 copy-start.5
  7.4 35.1 %partials.1.send_ref = bf16[16,528,128]{2,1,0:T(8,128)(2,1)S(1)} custom-call(s32[64,128]{1,0:T(8,128)S(1)} %bitcast.7, s32[128]{0:T(128)S(1)} %bitcast.9, bf16[64,128]{1,0:T(8,128)(2,1)S(1)} %collective-permute-done.low_ref, bf16[2048,128]{1,0:T(8,128)(2,1)S(1)} %copy-done, bf16[64,128]{1,0:T(8,128)(2,1)S(1)} %collective-permute-done.1.high_ref, ...), custom_call_target="tpu_custom_call" | custom-call | flops 805306368 | bytes 60000000 | tf_op jit(solution)/shard_map/partials/pallas_call | solution.py:120
  42.5 0.0 copy-done.5
  42.5 43.6 %exchange.1 = (bf16[1024,128]{1,0:T(8,128)(2,1)S(1)}, f32[32,1024]{1,0:T(8,128)S(1)}) custom-call(f32[8]{0:T(128)S(1)} %copy-done.5, bf16[16,528,128]{2,1,0:T(8,128)(2,1)S(1)} %partials.1.send_ref), custom_call_target="tpu_custom_call" | custom-call | tf_op jit(solution)/shard_map/exchange/pallas_call | solution.py:262
  86.2 0.7 copy.15
  86.9 0.7 copy.16
Async XLA Ops:
  1.4 6.0 %collective-permute-start.1 = (bf16[64,128]{1,0:T(8,128)(2,1)S(1)}, bf16[64,128]{1,0:T(8,128)(2,1)S(1)}, u32[]{:S(2)}, u32[]{:S(2)}) collective-permute-start(bf16[64,128]{1,0:T(8,128)(2,1)S(1)} %get-tuple-element.2), channel_id=1, source_target_pairs={{2,0},{4,2},{6,4},{8,6},{10,8},{12,10},{14,12},{16,14},{18,16},{20... | collective-permute-start | bytes 49160 | tf_op jit(solution)/shard_map/ppermute | solution.py:295
  1.6 5.7 %collective-permute-start = (bf16[64,128]{1,0:T(8,128)(2,1)S(1)}, bf16[64,128]{1,0:T(8,128)(2,1)S(1)}, u32[]{:S(2)}, u32[]{:S(2)}) collective-permute-start(bf16[64,128]{1,0:T(8,128)(2,1)S(1)} %get-tuple-element.3), channel_id=1, source_target_pairs={{0,2},{2,4},{4,6},{6,8},{8,10},{10,12},{12,14},{14,16},{16,18},{18... | collective-permute-start | bytes 49160 | tf_op jit(solution)/shard_map/ppermute | solution.py:294
  5.5 1.9 %copy-start = (bf16[2048,128]{1,0:T(8,128)(2,1)S(1)}, bf16[2048,128]{1,0:T(8,128)(2,1)}, u32[]{:S(2)}) copy-start(bf16[2048,128]{1,0:T(8,128)(2,1)} %field_ref.1) | copy-start | bytes 1572868
  5.5 1.9 %copy-start.1 = (f32[2,4,2048]{2,1,0:T(4,128)S(1)}, f32[2,4,2048]{2,1,0:T(4,128)}, u32[]{:S(2)}) copy-start(f32[2,4,2048]{2,1,0:T(4,128)} %coef_ref.1) | copy-start | bytes 196612
  5.5 1.9 %copy-start.2 = (s32[128,64]{0,1:T(8,128)S(1)}, s32[128,64]{0,1:T(8,128)}, u32[]{:S(2)}) copy-start(s32[128,64]{0,1:T(8,128)} %param.12) | copy-start | bytes 98308
  5.5 1.9 %copy-start.3 = (s32[2048,4]{0,1:T(4,128)S(1)}, s32[2048,4]{0,1:T(4,128)}, u32[]{:S(2)}) copy-start(s32[2048,4]{0,1:T(4,128)} %param.10) | copy-start | bytes 98308
  5.5 1.9 %copy-start.4 = (s32[128,1]{0,1:T(1,128)S(1)}, s32[128,1]{0,1:T(1,128)}, u32[]{:S(2)}) copy-start(s32[128,1]{0,1:T(1,128)} %param.14) | copy-start | bytes 1540
  7.4 35.1 %copy-start.5 = (f32[8]{0:T(128)S(1)}, f32[8]{0:T(128)}, u32[]{:S(2)}) copy-start(f32[8]{0:T(128)} %level_ref.1) | copy-start | bytes 100

commit v3 on v2

--- a/solution.py
+++ b/solution.py
@@ -16,6 +16,8 @@
 SUB = 8
 TILE = 128
 GROUP = LANES // TB
+PIECE = 32
+SPAN = SB + SUB
 MESH = pl.DeviceIdType.MESH
 
 
@@ -25,9 +27,9 @@
 
 def partial_kernel(
     capacity, src_count,
-    src_ref, dest_ref, low_ref, field_ref, high_ref, coef_ref, near_ref, tgt_ref, weight_ref,
+    src_ref, home_ref, low_ref, field_ref, high_ref, coef_ref, near_ref, tgt_ref, weight_ref,
     send_ref,
-    ext, recon, picked, tags, count, home,
+    ext, recon, picked, tags, mixes,
 ):
     cells, columns = field_ref.shape
     blocks = tgt_ref.shape[0]
@@ -42,22 +44,65 @@
     ext[HW:HW + cells, :] = field_ref[...]
     ext[HW + cells:HW + cells + HW, :] = high_ref[...]
 
-    @pl.loop(0, src_count)
-    def _(d):
-        count[d] = 0
-
     lane_group = lax.broadcasted_iota(jnp.int32, (1, LANES), 1) // TB
 
-    @pl.loop(0, blocks)
-    def _(b):
-        d = dest_ref[b]
-        rank = count[d]
-        count[d] = rank + 1
-        home[b] = d * capacity + rank
-        line = pl.ds(d * lines + rank // GROUP, 1)
+    @pl.loop(0, cells // TILE)
+    def _(t):
+        base = pl.multiple_of(t * TILE, TILE)
+        near = near_ref[:, pl.ds(base, TILE)] - base
+        coef = [coef_ref[g, :, pl.ds(base, TILE)] for g in range(2)]
+        totals = [-jnp.sum(coef[g], axis=0, keepdims=True) for g in range(2)]
+        held = ext[pl.ds(base, window), :]
+        rows = pl.multiple_of(base * SUB, TILE * SUB)
+        recon[pl.ds(rows, TILE, stride=SUB), :] = field_ref[pl.ds(base, TILE), :].astype(
+            jnp.float32
+        )
+        for w in range(0, window, PIECE):
+            here = lax.broadcasted_iota(jnp.int32, (PIECE, TILE), 0) + w
+            own = here == lax.broadcasted_iota(jnp.int32, (PIECE, TILE), 1) + HW
+            mixed = [jnp.where(own, totals[g], 0.0) for g in range(2)]
+            for k in range(near.shape[0]):
+                hit = here == near[k:k + 1, :]
+                for g in range(2):
+                    mixed[g] = mixed[g] + jnp.where(hit, coef[g][k:k + 1, :], 0.0)
+            for g in range(2):
+                high = mixed[g].astype(jnp.bfloat16)
+                rest = (mixed[g] - high.astype(jnp.float32)).astype(jnp.bfloat16)
+                mixes[w:w + PIECE, 2 * g * TILE:(2 * g + 1) * TILE] = high
+                mixes[w:w + PIECE, (2 * g + 1) * TILE:(2 * g + 2) * TILE] = rest
+        for g in range(2):
+            value = contract_first(mixes[:, 2 * g * TILE:(2 * g + 1) * TILE], held)
+            value = value + contract_first(mixes[:, (2 * g + 1) * TILE:(2 * g + 2) * TILE], held)
+            recon[pl.ds(rows + 1 + g, TILE, stride=SUB), :] = value
+
+    def one(b, buffer):
+        slot = home_ref[b]
+        for j in range(SB):
+            at = pl.multiple_of(src_ref[b, j], SUB)
+            to = (j % GROUP) * (SB // GROUP) + j // GROUP
+            buffer[pl.ds(to, 3, stride=SPAN), :] = recon[pl.ds(at, SUB), :][0:3, :]
+        held = weight_ref[b]
+        total = None
+        for q in range(GROUP):
+            parts = [
+                buffer[pl.ds(c * SPAN + q * (SB // GROUP), SB // GROUP), :] for c in range(3)
+            ]
+            rows = jnp.concatenate(parts, axis=0).astype(jnp.bfloat16)
+            product = contract_first(held[:, q * TB:(q + 1) * TB], rows)
+            total = product if total is None else total + product
+        owner = slot // capacity
+        rank = slot % capacity
+        row = pl.multiple_of(rank * TB, TB)
+        send_ref[owner, pl.ds(row, TB), :] = total.astype(jnp.bfloat16)
+        line = pl.ds(owner * lines + rank // GROUP, 1)
         tags[line, :] = jnp.where(
             lane_group == rank % GROUP, tgt_ref[pl.ds(b, 1), :], tags[line, :]
         )
+
+    @pl.loop(0, blocks // 2)
+    def _(n):
+        one(2 * n, picked.at[0])
+        one(2 * n + 1, picked.at[1])
 
     @pl.loop(0, src_count)
     def _(d):
@@ -65,53 +110,8 @@
         digits = jnp.concatenate([cell // 256, cell % 256], axis=0).astype(jnp.float32)
         send_ref[d, rows_each:, :] = digits.astype(jnp.bfloat16)
 
-    @pl.loop(0, cells // TILE)
-    def _(t):
-        base = pl.multiple_of(t * TILE, TILE)
-        near = near_ref[:, pl.ds(base, TILE)] - base
-        coef = [coef_ref[g, :, pl.ds(base, TILE)] for g in range(2)]
-        place_w = lax.broadcasted_iota(jnp.int32, (window, TILE), 0)
-        own = place_w == lax.broadcasted_iota(jnp.int32, (window, TILE), 1) + HW
-        hits = [place_w == near[k:k + 1, :] for k in range(near.shape[0])]
-        held = ext[pl.ds(base, window), :]
-        rows = pl.multiple_of(base * SUB, TILE * SUB)
-        recon[pl.ds(rows, TILE, stride=SUB), :] = field_ref[pl.ds(base, TILE), :].astype(
-            jnp.float32
-        )
-        for g in range(2):
-            total = -jnp.sum(coef[g], axis=0, keepdims=True)
-            mix = jnp.where(own, total, 0.0)
-            for k, hit in enumerate(hits):
-                mix = mix + jnp.where(hit, coef[g][k:k + 1, :], 0.0)
-            high = mix.astype(jnp.bfloat16)
-            rest = (mix - high.astype(jnp.float32)).astype(jnp.bfloat16)
-            value = contract_first(high, held) + contract_first(rest, held)
-            recon[pl.ds(rows + 1 + g, TILE, stride=SUB), :] = value
-
-    def one(b, buffer):
-        slot = home[b]
-        for j in range(SB):
-            at = pl.multiple_of(src_ref[j, b] * SUB, SUB)
-            buffer[j * SUB:(j + 1) * SUB, :] = recon[pl.ds(at, SUB), :]
-        held = weight_ref[b]
-        total = None
-        for q in range(GROUP):
-            parts = [
-                buffer[pl.ds(q * SUB + c, SB // GROUP, stride=GROUP * SUB), :] for c in range(3)
-            ]
-            rows = jnp.concatenate(parts, axis=0).astype(jnp.bfloat16)
-            product = contract_first(held[:, q * TB:(q + 1) * TB], rows)
-            total = product if total is None else total + product
-        row = pl.multiple_of(slot % capacity * TB, TB)
-        send_ref[slot // capacity, pl.ds(row, TB), :] = total.astype(jnp.bfloat16)
-
-    @pl.loop(0, blocks // 2)
-    def _(n):
-        one(2 * n, picked.at[0])
-        one(2 * n + 1, picked.at[1])
-
-
-def partials(capacity, src_count, src_t, dest, low, field, high, coef, near_t, tgt, weight):
+
+def partials(capacity, src_count, src_rows, home, low, field, high, coef, near_t, tgt, weight):
     cells, columns = field.shape
     blocks = tgt.shape[0]
     lines = -(-capacity // (GROUP * SUB)) * SUB
@@ -127,10 +127,9 @@
         scratch_shapes=[
             pltpu.VMEM((cells + 2 * HW, columns), jnp.bfloat16),
             pltpu.VMEM((cells * SUB, columns), jnp.float32),
-            pltpu.VMEM((2, SB * SUB, columns), jnp.float32),
+            pltpu.VMEM((2, 3 * SPAN, columns), jnp.float32),
             pltpu.VMEM((src_count * lines, LANES), jnp.int32),
-            pltpu.SMEM((src_count,), jnp.int32),
-            pltpu.SMEM((blocks,), jnp.int32),
+            pltpu.VMEM((TILE + 2 * HW, 4 * TILE), jnp.bfloat16),
         ],
         compiler_params=pltpu.CompilerParams(vmem_limit_bytes=40 << 20),
         cost_estimate=pl.CostEstimate(
@@ -139,7 +138,7 @@
             transcendentals=0,
         ),
         name="partials",
-    )(src_t, dest, low, field, high, coef, near_t, tgt, weight)
+    )(src_rows, home, low, field, high, coef, near_t, tgt, weight)
 
 
 def exchange_kernel(
@@ -296,9 +295,13 @@
     columns = field.shape[1]
     blocks = src_index.shape[0]
     capacity = 2 * blocks // src_count
+    owner = block_dest[:, 0]
+    order = jnp.arange(blocks, dtype=jnp.int32)
+    earlier = (owner[:, None] == owner[None, :]) & (order[:, None] < order[None, :])
+    home = owner * capacity + jnp.sum(earlier.astype(jnp.int32), axis=0)
     shaped = weights.reshape(blocks, 3 * SB * TB // LANES, LANES)
     sent = partials(
-        capacity, src_count, src_index.T, block_dest[:, 0], low, field, high, grad_coef,
+        capacity, src_count, src_index * SUB, home, low, field, high, grad_coef,
         neighbours.T, jnp.tile(tgt_index, (1, GROUP)), shaped,
     )
     return exchange(

time: 88 us -> 82.3 us (0.935)
  Pallas kernels: 78.7 us -> 70.7 us
  other arithmetic: 0 us -> 1.49 us
    pallas_call x1, Pallas kernels: 35.1 us -> 27.1 us  [partials(): pl.pallas_call(functools.partial(partial_kernel, capacity, src_count), ou...]
    unnamed x15 -> x12, local copies, waits for them, and re-layouts: 3.21 us -> 4.05 us
  transfers between devices with their start and end apart: 2 -> 2, of which waited for: 0 -> 0; matrix products, arithmetic and copies ran while one was open for 3% -> 6% of each run, Pallas kernels for 0% -> 0%
where the time goes in v3:
time: 82.3 us; the launch traced here: 81.8 us
  Pallas kernels  70.7 us (86%)
  local copies, waits for them, and re-layouts  5.6 us (7%)
  starting transfers between devices  3.26 us (4%)
  other arithmetic  1.49 us (2%)
    pallas_call x1, Pallas kernels, exchange(): pl.pallas_call(functools.partial(exchange_kernel, count, level_count, lev...  43.6 us
    pallas_call x1, Pallas kernels, partials(): pl.pallas_call(functools.partial(partial_kernel, capacity, src_count), ou...  27.1 us
    unnamed x12, local copies, waits for them, and re-layouts  4.05 us
    ppermute x1, starting transfers between devices, shards(): low = lax.ppermute(field[-HW:], 'src', forward)  3.01 us
  transfers between devices with their start and end apart: 2, of which 0 were waited for; matrix products, arithmetic and copies ran while one was open for 6% of the time, Pallas kernels for 0%

profile of v3, /device:TPU:15, one launch (start us, length us, event | category | flops | bytes accessed | tf_op | source)
XLA Modules:
  0.0 81.8 jit_solution(14961983275191905091)
XLA Ops:
  0.6 0.7 fusion.1
  1.4 0.3 collective-permute-start.1
  1.6 3.0 %collective-permute-start = (bf16[64,128]{1,0:T(8,128)(2,1)S(1)}, bf16[64,128]{1,0:T(8,128)(2,1)S(1)}, u32[]{:S(2)}, u32[]{:S(2)}) collective-permute-start(bf16[64,128]{1,0:T(8,128)(2,1)S(1)} %get-tuple-element.3), channel_id=1, source_target_pairs={{0,2},{2,4},{4,6},{6,8},{8,10},{10,12},{12,14},{14,16},{16,18},{18... | collective-permute-start | bytes 49160 | tf_op jit(solution)/shard_map/ppermute | solution.py:293
  4.6 0.8 %convert_reduce_fusion = s32[128]{0:T(128)S(1)} fusion(s32[128]{0:T(128)} %bitcast.10), kind=kLoop, calls=%fused_computation | loop fusion | flops 81792 | bytes 1024 | tf_op jit(solution)/shard_map/reduce_sum | solution.py:301
  5.5 0.9 %copy.16 = s32[128,64]{1,0:T(8,128)S(1)} copy(s32[128,64]{0,1:T(8,128)} %param.12) | data formatting | bytes 65536 | tf_op args[4]
  6.3 0.7 multiply_add_fusion.home_ref
  7.0 0.7 tile.4
  7.7 0.1 copy.18.tgt_ref
  7.8 0.0 copy-start
  7.8 0.0 copy-start.1
  7.8 0.0 copy-start.2
  7.8 1.8 %copy.19 = bf16[16,8,48,128]{3,2,1,0:T(8,128)(2,1)S(1)} copy(bf16[16,8,48,128]{3,1,2,0:T(8,128)(2,1)} %bitcast.8) | data formatting | bytes 3145728
  9.7 0.0 collective-permute-done.1.high_ref
  9.7 0.0 collective-permute-done.low_ref
  9.7 0.0 copy-done
  9.7 0.0 copy-done.1
  9.7 0.0 copy-done.2
  9.7 0.0 copy-start.3
  9.7 27.1 %partials.1.send_ref = bf16[16,528,128]{2,1,0:T(8,128)(2,1)S(1)} custom-call(s32[128,64]{1,0:T(8,128)S(1)} %broadcast_multiply_fusion.src_ref, s32[128]{0:T(128)S(1)} %multiply_add_fusion.home_ref, bf16[64,128]{1,0:T(8,128)(2,1)S(1)} %collective-permute-done.low_ref, bf16[2048,128]{1,0:T(8,128)(2,1)S(1)} %copy-done, ...), custom_call_target="tpu_custom_call" | custom-call | flops 805306368 | bytes 60000000 | tf_op jit(solution)/shard_map/partials/pallas_call | solution.py:120
  36.8 0.0 copy-done.3
  36.8 43.6 %exchange.1 = (bf16[1024,128]{1,0:T(8,128)(2,1)S(1)}, f32[32,1024]{1,0:T(8,128)S(1)}) custom-call(f32[8]{0:T(128)S(1)} %copy-done.3, bf16[16,528,128]{2,1,0:T(8,128)(2,1)S(1)} %partials.1.send_ref), custom_call_target="tpu_custom_call" | custom-call | tf_op jit(solution)/shard_map/exchange/pallas_call | solution.py:261
  80.4 0.7 copy.22
  81.1 0.7 copy.23
  (1 shorter events, 0.0 us)
Async XLA Ops:
  1.4 8.3 %collective-permute-start.1 = (bf16[64,128]{1,0:T(8,128)(2,1)S(1)}, bf16[64,128]{1,0:T(8,128)(2,1)S(1)}, u32[]{:S(2)}, u32[]{:S(2)}) collective-permute-start(bf16[64,128]{1,0:T(8,128)(2,1)S(1)} %get-tuple-element.2), channel_id=1, source_target_pairs={{2,0},{4,2},{6,4},{8,6},{10,8},{12,10},{14,12},{16,14},{18,16},{20... | collective-permute-start | bytes 49160 | tf_op jit(solution)/shard_map/ppermute | solution.py:294
  1.6 8.1 %collective-permute-start = (bf16[64,128]{1,0:T(8,128)(2,1)S(1)}, bf16[64,128]{1,0:T(8,128)(2,1)S(1)}, u32[]{:S(2)}, u32[]{:S(2)}) collective-permute-start(bf16[64,128]{1,0:T(8,128)(2,1)S(1)} %get-tuple-element.3), channel_id=1, source_target_pairs={{0,2},{2,4},{4,6},{6,8},{8,10},{10,12},{12,14},{14,16},{16,18},{18... | collective-permute-start | bytes 49160 | tf_op jit(solution)/shard_map/ppermute | solution.py:293
  7.8 1.9 %copy-start = (bf16[2048,128]{1,0:T(8,128)(2,1)S(1)}, bf16[2048,128]{1,0:T(8,128)(2,1)}, u32[]{:S(2)}) copy-start(bf16[2048,128]{1,0:T(8,128)(2,1)} %field_ref.1) | copy-start | bytes 1572868
  7.8 1.9 %copy-start.1 = (f32[2,4,2048]{2,1,0:T(4,128)S(1)}, f32[2,4,2048]{2,1,0:T(4,128)}, u32[]{:S(2)}) copy-start(f32[2,4,2048]{2,1,0:T(4,128)} %coef_ref.1) | copy-start | bytes 196612
  7.8 1.9 %copy-start.2 = (s32[2048,4]{0,1:T(4,128)S(1)}, s32[2048,4]{0,1:T(4,128)}, u32[]{:S(2)}) copy-start(s32[2048,4]{0,1:T(4,128)} %param.10) | copy-start | bytes 98308
  9.7 27.1 %copy-start.3 = (f32[8]{0:T(128)S(1)}, f32[8]{0:T(128)}, u32[]{:S(2)}) copy-start(f32[8]{0:T(128)} %level_ref.1) | copy-start | bytes 100

commit v4 on v3

--- a/solution.py
+++ b/solution.py
@@ -16,18 +16,25 @@
 SUB = 8
 TILE = 128
 GROUP = LANES // TB
+GROUP_BITS = GROUP.bit_length() - 1
 PIECE = 32
+UNROLL = 4
+BATCH = 16
 SPAN = SB + SUB
 MESH = pl.DeviceIdType.MESH
 
 
+def tag_lines(capacity):
+    return -(-capacity // (GROUP * SUB)) * SUB
+
+
 def contract_first(a, b):
     return lax.dot_general(a, b, (((0,), (0,)), ((), ())), preferred_element_type=jnp.float32)
 
 
 def partial_kernel(
     capacity, src_count,
-    src_ref, home_ref, low_ref, field_ref, high_ref, coef_ref, near_ref, tgt_ref, weight_ref,
+    src_ref, row_ref, tag_ref, low_ref, field_ref, high_ref, coef_ref, near_ref, tgt_ref, weight_ref,
     send_ref,
     ext, recon, picked, tags, mixes,
 ):
@@ -76,11 +83,14 @@
             recon[pl.ds(rows + 1 + g, TILE, stride=SUB), :] = value
 
     def one(b, buffer):
-        slot = home_ref[b]
-        for j in range(SB):
-            at = pl.multiple_of(src_ref[b, j], SUB)
-            to = (j % GROUP) * (SB // GROUP) + j // GROUP
-            buffer[pl.ds(to, 3, stride=SPAN), :] = recon[pl.ds(at, SUB), :][0:3, :]
+        index = src_ref.at[b]
+        for begin in range(0, SB, BATCH):
+            found = [
+                recon[pl.ds(pl.multiple_of(index[begin + j], SUB), SUB), :] for j in range(BATCH)
+            ]
+            for j in range(BATCH):
+                to = ((begin + j) % GROUP) * (SB // GROUP) + (begin + j) // GROUP
+                buffer[pl.ds(to, 3, stride=SPAN), :] = found[j][0:3, :]
         held = weight_ref[b]
         total = None
         for q in range(GROUP):
@@ -90,44 +100,43 @@
             rows = jnp.concatenate(parts, axis=0).astype(jnp.bfloat16)
             product = contract_first(held[:, q * TB:(q + 1) * TB], rows)
             total = product if total is None else total + product
-        owner = slot // capacity
-        rank = slot % capacity
-        row = pl.multiple_of(rank * TB, TB)
-        send_ref[owner, pl.ds(row, TB), :] = total.astype(jnp.bfloat16)
-        line = pl.ds(owner * lines + rank // GROUP, 1)
+        send_ref[pl.ds(pl.multiple_of(row_ref[b], TB // 2), TB), :] = total.astype(jnp.bfloat16)
+        tag = tag_ref[b]
+        line = pl.ds(lax.shift_right_logical(tag, GROUP_BITS), 1)
         tags[line, :] = jnp.where(
-            lane_group == rank % GROUP, tgt_ref[pl.ds(b, 1), :], tags[line, :]
+            lane_group == jnp.bitwise_and(tag, GROUP - 1), tgt_ref[pl.ds(b, 1), :], tags[line, :]
         )
 
-    @pl.loop(0, blocks // 2)
+    @pl.loop(0, blocks // UNROLL)
     def _(n):
-        one(2 * n, picked.at[0])
-        one(2 * n + 1, picked.at[1])
+        for m in range(UNROLL):
+            one(UNROLL * n + m, picked.at[m])
 
     @pl.loop(0, src_count)
     def _(d):
         cell = tags[pl.ds(pl.multiple_of(d * lines, SUB), lines), :]
         digits = jnp.concatenate([cell // 256, cell % 256], axis=0).astype(jnp.float32)
-        send_ref[d, rows_each:, :] = digits.astype(jnp.bfloat16)
-
-
-def partials(capacity, src_count, src_rows, home, low, field, high, coef, near_t, tgt, weight):
+        at = pl.multiple_of(d * (rows_each + 2 * lines) + rows_each, 2 * SUB)
+        send_ref[pl.ds(at, 2 * lines), :] = digits.astype(jnp.bfloat16)
+
+
+def partials(capacity, src_count, src_rows, home_row, home_tag, low, field, high, coef, near_t, tgt, weight):
     cells, columns = field.shape
     blocks = tgt.shape[0]
-    lines = -(-capacity // (GROUP * SUB)) * SUB
+    lines = tag_lines(capacity)
     smem = pl.BlockSpec(memory_space=pltpu.SMEM)
     vmem = pl.BlockSpec(memory_space=pltpu.VMEM)
     return pl.pallas_call(
         functools.partial(partial_kernel, capacity, src_count),
         out_shape=jax.ShapeDtypeStruct(
-            (src_count, capacity * TB + 2 * lines, columns), jnp.bfloat16
+            (src_count * (capacity * TB + 2 * lines), columns), jnp.bfloat16
         ),
-        in_specs=[smem, smem] + [vmem] * 7,
+        in_specs=[smem] * 3 + [vmem] * 7,
         out_specs=vmem,
         scratch_shapes=[
             pltpu.VMEM((cells + 2 * HW, columns), jnp.bfloat16),
             pltpu.VMEM((cells * SUB, columns), jnp.float32),
-            pltpu.VMEM((2, 3 * SPAN, columns), jnp.float32),
+            pltpu.VMEM((UNROLL, 3 * SPAN, columns), jnp.float32),
             pltpu.VMEM((src_count * lines, LANES), jnp.int32),
             pltpu.VMEM((TILE + 2 * HW, 4 * TILE), jnp.bfloat16),
         ],
@@ -138,7 +147,7 @@
             transcendentals=0,
         ),
         name="partials",
-    )(src_rows, home, low, field, high, coef, near_t, tgt, weight)
+    )(src_rows, home_row, home_tag, low, field, high, coef, near_t, tgt, weight)
 
 
 def exchange_kernel(
@@ -298,14 +307,17 @@
     owner = block_dest[:, 0]
     order = jnp.arange(blocks, dtype=jnp.int32)
     earlier = (owner[:, None] == owner[None, :]) & (order[:, None] < order[None, :])
-    home = owner * capacity + jnp.sum(earlier.astype(jnp.int32), axis=0)
+    rank = jnp.sum(earlier.astype(jnp.int32), axis=0)
+    lines = tag_lines(capacity)
+    home_row = owner * (capacity * TB + 2 * lines) + rank * TB
+    home_tag = owner * (lines * GROUP) + rank
     shaped = weights.reshape(blocks, 3 * SB * TB // LANES, LANES)
     sent = partials(
-        capacity, src_count, src_index * SUB, home, low, field, high, grad_coef,
+        capacity, src_count, src_index * SUB, home_row, home_tag, low, field, high, grad_coef,
         neighbours.T, jnp.tile(tgt_index, (1, GROUP)), shaped,
     )
     return exchange(
-        level_weight, sent, capacity * TB, src_count, lax.axis_size("lev"), columns // FIELDS
+        level_weight, sent.reshape(src_count, -1, columns), capacity * TB, src_count, lax.axis_size("lev"), columns // FIELDS
     )
 
 

time: 82.3 us -> 77 us (0.936)
  Pallas kernels: 70.7 us -> 65.5 us
    pallas_call x1, Pallas kernels: 27.1 us -> 21.8 us  [partials(): pl.pallas_call(functools.partial(partial_kernel, capacity, src_count), ou...]
where the time goes in v4:
time: 77 us; the launch traced here: 76.6 us
  Pallas kernels  65.5 us (85%)
  local copies, waits for them, and re-layouts  5.6 us (7%)
  starting transfers between devices  3.26 us (4%)
  other arithmetic  1.5 us (2%)
    pallas_call x1, Pallas kernels, exchange(): pl.pallas_call(functools.partial(exchange_kernel, count, level_count, lev...  43.6 us
    pallas_call x1, Pallas kernels, partials(): pl.pallas_call(functools.partial(partial_kernel, capacity, src_count), ou...  21.8 us
    unnamed x12, local copies, waits for them, and re-layouts  4.05 us
    ppermute x1, starting transfers between devices, shards(): low = lax.ppermute(field[-HW:], 'src', forward)  3.01 us
  transfers between devices with their start and end apart: 2, of which 0 were waited for; matrix products, arithmetic and copies ran while one was open for 6% of the time, Pallas kernels for 0%

profile of v4, /device:TPU:15, one launch (start us, length us, event | category | flops | bytes accessed | tf_op | source)
XLA Modules:
  0.0 76.6 jit_solution(12782685886804107760)
XLA Ops:
  0.6 0.7 fusion.1
  1.4 0.3 collective-permute-start.1
  1.6 3.0 %collective-permute-start = (bf16[64,128]{1,0:T(8,128)(2,1)S(1)}, bf16[64,128]{1,0:T(8,128)(2,1)S(1)}, u32[]{:S(2)}, u32[]{:S(2)}) collective-permute-start(bf16[64,128]{1,0:T(8,128)(2,1)S(1)} %get-tuple-element.3), channel_id=1, source_target_pairs={{0,2},{2,4},{4,6},{6,8},{8,10},{10,12},{12,14},{14,16},{16,18},{18... | collective-permute-start | bytes 49160 | tf_op jit(solution)/shard_map/ppermute | solution.py:302
  4.6 0.8 %convert_reduce_fusion = s32[128]{0:T(128)S(1)} fusion(s32[128]{0:T(128)} %bitcast.13), kind=kLoop, calls=%fused_computation | loop fusion | flops 81792 | bytes 1024 | tf_op jit(solution)/shard_map/reduce_sum | solution.py:310
  5.5 0.9 %copy.16 = s32[128,64]{1,0:T(8,128)S(1)} copy(s32[128,64]{0,1:T(8,128)} %param.12) | data formatting | bytes 65536 | tf_op args[4]
  6.3 0.7 multiply_add_fusion
  7.0 0.7 tile.4
  7.7 0.1 copy.18.tgt_ref
  7.8 0.0 copy-start
  7.8 0.0 copy-start.1
  7.8 0.0 copy-start.2
  7.8 1.8 %copy.19 = bf16[16,8,48,128]{3,2,1,0:T(8,128)(2,1)S(1)} copy(bf16[16,8,48,128]{3,1,2,0:T(8,128)(2,1)} %bitcast.11) | data formatting | bytes 3145728
  9.7 0.0 collective-permute-done.1.high_ref
  9.7 0.0 collective-permute-done.low_ref
  9.7 0.0 copy-done
  9.7 0.0 copy-done.1
  9.7 0.0 copy-done.2
  9.7 0.0 copy-start.3
  9.7 21.8 %partials.1 = bf16[8448,128]{1,0:T(8,128)(2,1)S(1)} custom-call(s32[128,64]{1,0:T(8,128)S(1)} %broadcast_multiply_fusion.src_ref, s32[128]{0:T(128)S(1)} %get-tuple-element.5.row_ref, s32[128]{0:T(128)S(1)} %get-tuple-element.4.tag_ref, bf16[64,128]{1,0:T(8,128)(2,1)S(1)} %collective-permute-done.low_ref, bf16[2048,128]{1,0:T(8,128)(2,1)S(1)} %copy-done, ...), custom_call_target="tpu_custom_call" | custom-call | flops 805306368 | bytes 60000000 | tf_op jit(solution)/shard_map/partials/pallas_call | solution.py:129
  31.6 0.0 copy-done.3
  31.6 43.6 %exchange.1 = (bf16[1024,128]{1,0:T(8,128)(2,1)S(1)}, f32[32,1024]{1,0:T(8,128)S(1)}) custom-call(f32[8]{0:T(128)S(1)} %copy-done.3, bf16[16,528,128]{2,1,0:T(8,128)(2,1)S(1)} %bitcast.8), custom_call_target="tpu_custom_call" | custom-call | tf_op jit(solution)/shard_map/exchange/pallas_call | solution.py:270
  75.2 0.7 copy.22
  75.9 0.7 copy.23
  (1 shorter events, 0.0 us)
Async XLA Ops:
  1.4 8.3 %collective-permute-start.1 = (bf16[64,128]{1,0:T(8,128)(2,1)S(1)}, bf16[64,128]{1,0:T(8,128)(2,1)S(1)}, u32[]{:S(2)}, u32[]{:S(2)}) collective-permute-start(bf16[64,128]{1,0:T(8,128)(2,1)S(1)} %get-tuple-element.2), channel_id=1, source_target_pairs={{2,0},{4,2},{6,4},{8,6},{10,8},{12,10},{14,12},{16,14},{18,16},{20... | collective-permute-start | bytes 49160 | tf_op jit(solution)/shard_map/ppermute | solution.py:303
  1.6 8.1 %collective-permute-start = (bf16[64,128]{1,0:T(8,128)(2,1)S(1)}, bf16[64,128]{1,0:T(8,128)(2,1)S(1)}, u32[]{:S(2)}, u32[]{:S(2)}) collective-permute-start(bf16[64,128]{1,0:T(8,128)(2,1)S(1)} %get-tuple-element.3), channel_id=1, source_target_pairs={{0,2},{2,4},{4,6},{6,8},{8,10},{10,12},{12,14},{14,16},{16,18},{18... | collective-permute-start | bytes 49160 | tf_op jit(solution)/shard_map/ppermute | solution.py:302
  7.8 1.9 %copy-start = (bf16[2048,128]{1,0:T(8,128)(2,1)S(1)}, bf16[2048,128]{1,0:T(8,128)(2,1)}, u32[]{:S(2)}) copy-start(bf16[2048,128]{1,0:T(8,128)(2,1)} %field_ref.1) | copy-start | bytes 1572868
  7.8 1.9 %copy-start.1 = (f32[2,4,2048]{2,1,0:T(4,128)S(1)}, f32[2,4,2048]{2,1,0:T(4,128)}, u32[]{:S(2)}) copy-start(f32[2,4,2048]{2,1,0:T(4,128)} %coef_ref.1) | copy-start | bytes 196612
  7.8 1.9 %copy-start.2 = (s32[2048,4]{0,1:T(4,128)S(1)}, s32[2048,4]{0,1:T(4,128)}, u32[]{:S(2)}) copy-start(s32[2048,4]{0,1:T(4,128)} %param.10) | copy-start | bytes 98308
  9.7 21.9 %copy-start.3 = (f32[8]{0:T(128)S(1)}, f32[8]{0:T(128)}, u32[]{:S(2)}) copy-start(f32[8]{0:T(128)} %level_ref.1) | copy-start | bytes 100

commit v5 on v4

--- a/solution.py
+++ b/solution.py
@@ -32,29 +32,20 @@
     return lax.dot_general(a, b, (((0,), (0,)), ((), ())), preferred_element_type=jnp.float32)
 
 
-def partial_kernel(
-    capacity, src_count,
-    src_ref, row_ref, tag_ref, low_ref, field_ref, high_ref, coef_ref, near_ref, tgt_ref, weight_ref,
-    send_ref,
-    ext, recon, picked, tags, mixes,
-):
-    cells, columns = field_ref.shape
-    blocks = tgt_ref.shape[0]
-    rows_each = capacity * TB
-    lines = tags.shape[0] // src_count
+def prepare_kernel(count, field_ref, coef_ref, near_ref, recon, ext, mixes, out_sem, in_sem):
+    cells = field_ref.shape[0]
     window = TILE + 2 * HW
-
-    send_ref[...] = jnp.zeros_like(send_ref)
-    tags[...] = jnp.zeros_like(tags)
-
-    ext[0:HW, :] = low_ref[...]
+    tiles = cells // TILE
+    me = lax.axis_index("src")
+    lev = lax.axis_index("lev")
+    right = lax.rem(me + 1, count)
+    left = lax.rem(me + count - 1, count)
+    barrier = pltpu.get_barrier_semaphore()
+    for other in (left, right):
+        pl.semaphore_signal(barrier, inc=1, device_id=(other, lev), device_id_type=MESH)
     ext[HW:HW + cells, :] = field_ref[...]
-    ext[HW + cells:HW + cells + HW, :] = high_ref[...]
-
-    lane_group = lax.broadcasted_iota(jnp.int32, (1, LANES), 1) // TB
-
-    @pl.loop(0, cells // TILE)
-    def _(t):
+
+    def tile(t):
         base = pl.multiple_of(t * TILE, TILE)
         near = near_ref[:, pl.ds(base, TILE)] - base
         coef = [coef_ref[g, :, pl.ds(base, TILE)] for g in range(2)]
@@ -82,6 +73,72 @@
             value = value + contract_first(mixes[:, (2 * g + 1) * TILE:(2 * g + 2) * TILE], held)
             recon[pl.ds(rows + 1 + g, TILE, stride=SUB), :] = value
 
+    @pl.loop(1, tiles // 2)
+    def _(t):
+        tile(t)
+
+    pl.semaphore_wait(barrier, 2)
+    low = pltpu.make_async_remote_copy(
+        src_ref=field_ref.at[pl.ds(cells - HW, HW)], dst_ref=ext.at[pl.ds(0, HW)],
+        send_sem=out_sem.at[0], recv_sem=in_sem.at[0],
+        device_id=(right, lev), device_id_type=MESH,
+    )
+    high = pltpu.make_async_remote_copy(
+        src_ref=field_ref.at[pl.ds(0, HW)], dst_ref=ext.at[pl.ds(HW + cells, HW)],
+        send_sem=out_sem.at[1], recv_sem=in_sem.at[1],
+        device_id=(left, lev), device_id_type=MESH,
+    )
+    low.start()
+    high.start()
+
+    @pl.loop(tiles // 2, tiles - 1)
+    def _(t):
+        tile(t)
+
+    low.wait()
+    high.wait()
+
+    @pl.loop(0, 2)
+    def _(e):
+        tile(e * (tiles - 1))
+
+
+def prepare(count, field, coef, near_t):
+    cells, columns = field.shape
+    vmem = pl.BlockSpec(memory_space=pltpu.VMEM)
+    return pl.pallas_call(
+        functools.partial(prepare_kernel, count),
+        out_shape=jax.ShapeDtypeStruct((cells * SUB, columns), jnp.float32),
+        in_specs=[vmem] * 3,
+        out_specs=vmem,
+        scratch_shapes=[
+            pltpu.VMEM((cells + 2 * HW, columns), jnp.bfloat16),
+            pltpu.VMEM((TILE + 2 * HW, 4 * TILE), jnp.bfloat16),
+            pltpu.SemaphoreType.DMA((2,)),
+            pltpu.SemaphoreType.DMA((2,)),
+        ],
+        compiler_params=pltpu.CompilerParams(
+            vmem_limit_bytes=24 << 20, collective_id=1, has_side_effects=True
+        ),
+        name="prepare",
+    )(field, coef, near_t)
+
+
+def partial_kernel(
+    capacity, src_count,
+    src_ref, row_ref, tag_ref, recon, tgt_ref, weight_ref,
+    send_ref,
+    picked, tags,
+):
+    blocks = tgt_ref.shape[0]
+    rows_each = capacity * TB
+    lines = tags.shape[0] // src_count
+
+    send_ref[...] = jnp.zeros_like(send_ref)
+    tags[...] = jnp.zeros_like(tags)
+
+    lane_group = lax.broadcasted_iota(jnp.int32, (1, LANES), 1) // TB
+
     def one(b, buffer):
         index = src_ref.at[b]
         for begin in range(0, SB, BATCH):
@@ -120,8 +177,8 @@
         send_ref[pl.ds(at, 2 * lines), :] = digits.astype(jnp.bfloat16)
 
 
-def partials(capacity, src_count, src_rows, home_row, home_tag, low, field, high, coef, near_t, tgt, weight):
-    cells, columns = field.shape
+def partials(capacity, src_count, src_rows, home_row, home_tag, recon, tgt, weight):
+    columns = recon.shape[1]
     blocks = tgt.shape[0]
     lines = tag_lines(capacity)
     smem = pl.BlockSpec(memory_space=pltpu.SMEM)
@@ -131,23 +188,20 @@
         out_shape=jax.ShapeDtypeStruct(
             (src_count * (capacity * TB + 2 * lines), columns), jnp.bfloat16
         ),
-        in_specs=[smem] * 3 + [vmem] * 7,
+        in_specs=[smem] * 3 + [vmem] * 3,
         out_specs=vmem,
         scratch_shapes=[
-            pltpu.VMEM((cells + 2 * HW, columns), jnp.bfloat16),
-            pltpu.VMEM((cells * SUB, columns), jnp.float32),
             pltpu.VMEM((UNROLL, 3 * SPAN, columns), jnp.float32),
             pltpu.VMEM((src_count * lines, LANES), jnp.int32),
-            pltpu.VMEM((TILE + 2 * HW, 4 * TILE), jnp.bfloat16),
         ],
-        compiler_params=pltpu.CompilerParams(vmem_limit_bytes=40 << 20),
+        compiler_params=pltpu.CompilerParams(vmem_limit_bytes=24 << 20),
         cost_estimate=pl.CostEstimate(
             flops=8 * blocks * SB * 3 * TB * columns,
             bytes_accessed=60_000_000,
             transcendentals=0,
         ),
         name="partials",
-    )(src_rows, home_row, home_tag, low, field, high, coef, near_t, tgt, weight)
+    )(src_rows, home_row, home_tag, recon, tgt, weight)
 
 
 def exchange_kernel(
@@ -297,10 +351,6 @@
 
 def shards(field, grad_coef, neighbours, level_weight, src_index, tgt_index, block_dest, weights):
     src_count = lax.axis_size("src")
-    forward = [(i, (i + 1) % src_count) for i in range(src_count)]
-    backward = [(target, source) for source, target in forward]
-    low = lax.ppermute(field[-HW:], "src", forward)
-    high = lax.ppermute(field[:HW], "src", backward)
     columns = field.shape[1]
     blocks = src_index.shape[0]
     capacity = 2 * blocks // src_count
@@ -313,8 +363,8 @@
     home_tag = owner * (lines * GROUP) + rank
     shaped = weights.reshape(blocks, 3 * SB * TB // LANES, LANES)
     sent = partials(
-        capacity, src_count, src_index * SUB, home_row, home_tag, low, field, high, grad_coef,
-        neighbours.T, jnp.tile(tgt_index, (1, GROUP)), shaped,
+        capacity, src_count, src_index * SUB, home_row, home_tag,
+        prepare(src_count, field, grad_coef, neighbours.T), jnp.tile(tgt_index, (1, GROUP)), shaped,
     )
     return exchange(
         level_weight, sent.reshape(src_count, -1, columns), capacity * TB, src_count, lax.axis_size("lev"), columns // FIELDS

time: 77 us -> 69.8 us (0.906)
  starting transfers between devices: 3.26 us -> 0 us
  Pallas kernels: 65.5 us -> 62.5 us
  local copies, waits for them, and re-layouts: 5.6 us -> 4.8 us
    pallas_call x0 -> x1, Pallas kernels: none -> 6.94 us  [prepare(): pl.pallas_call(functools.partial(prepare_kernel, count), out_shape=jax.Sh...]
    pallas_call x1, Pallas kernels: 21.8 us -> 15.1 us  [partials(): pl.pallas_call(functools.partial(partial_kernel, capacity, src_count), ou...]
    ppermute x2 -> x0, starting transfers between devices: 3.26 us -> none  [the longest x1 3.01 us: shards(): low = lax.ppermute(field[-HW:], 'src', forward)]
    pallas_call x1, Pallas kernels: 43.6 us -> 40.5 us  [exchange(): pl.pallas_call(functools.partial(exchange_kernel, count, level_count, lev...]
  transfers between devices with their start and end apart: 2 -> 0, of which waited for: 0 -> 0; matrix products, arithmetic and copies ran while one was open for 6% -> 0% of each run, Pallas kernels for 0% -> 0%
where the time goes in v5:
time: 69.8 us; the launch traced here: 69.6 us
  Pallas kernels  62.5 us (90%)
  local copies, waits for them, and re-layouts  4.8 us (7%)
  other arithmetic  1.5 us (2%)
  between operations  0.75 us (1%)
    pallas_call x1, Pallas kernels, exchange(): pl.pallas_call(functools.partial(exchange_kernel, count, level_count, lev...  40.5 us
    pallas_call x1, Pallas kernels, partials(): pl.pallas_call(functools.partial(partial_kernel, capacity, src_count), ou...  15.1 us
    pallas_call x1, Pallas kernels, prepare(): pl.pallas_call(functools.partial(prepare_kernel, count), out_shape=jax.Sh...  6.94 us
    unnamed x12, local copies, waits for them, and re-layouts  3.98 us

profile of v5, /device:TPU:15, one launch (start us, length us, event | category | flops | bytes accessed | tf_op | source)
XLA Modules:
  0.0 69.6 jit_solution(2908278349341311185)
XLA Ops:
  0.6 0.0 copy-start.2
  0.6 0.0 copy-start.1
  0.6 0.0 copy-start
  0.7 0.8 %convert_reduce_fusion = s32[128]{0:T(128)S(1)} fusion(s32[128]{0:T(128)} %bitcast.13), kind=kLoop, calls=%fused_computation | loop fusion | flops 81792 | bytes 1024 | tf_op jit(solution)/shard_map/reduce_sum | solution.py:360
  1.5 0.7 multiply_add_fusion
  2.2 0.8 %copy.16 = s32[128,64]{1,0:T(8,128)S(1)} copy(s32[128,64]{0,1:T(8,128)} %param.12) | data formatting | bytes 65536 | tf_op args[4]
  3.0 0.7 %tile.4 = s32[128,4,32]{0,2,1:T(8,128)S(1)} broadcast(s32[128,32]{0,1:T(8,128)} %param.13), dimensions={0,2} | broadcast | bytes 81920 | tf_op jit(solution)/shard_map/tile | solution.py:367
  3.7 0.1 copy.18.tgt_ref
  3.8 1.8 %copy.19 = bf16[16,8,48,128]{3,2,1,0:T(8,128)(2,1)S(1)} copy(bf16[16,8,48,128]{3,1,2,0:T(8,128)(2,1)} %bitcast.11) | data formatting | bytes 3145728
  5.6 0.0 copy-done.2
  5.6 0.0 copy-done.1
  5.6 0.0 copy-done
  5.6 6.9 %prepare.1.recon = f32[16384,128]{1,0:T(8,128)S(1)} custom-call(bf16[2048,128]{1,0:T(8,128)(2,1)S(1)} %copy-done, f32[2,4,2048]{2,1,0:T(4,128)S(1)} %copy-done.1, s32[4,2048]{1,0:T(4,128)S(1)} %bitcast.10), custom_call_target="tpu_custom_call" | custom-call | tf_op jit(solution)/shard_map/prepare/pallas_call | solution.py:109
  12.6 0.0 copy-start.3
  12.6 15.1 %partials.1 = bf16[8448,128]{1,0:T(8,128)(2,1)S(1)} custom-call(s32[128,64]{1,0:T(8,128)S(1)} %broadcast_multiply_fusion.src_ref, s32[128]{0:T(128)S(1)} %get-tuple-element.3.row_ref, s32[128]{0:T(128)S(1)} %get-tuple-element.2.tag_ref, f32[16384,128]{1,0:T(8,128)S(1)} %prepare.1.recon, s32[128,128]{1,0:T(8,128)S(1)} %copy.18.tgt_ref, ...), custom_call_target="tpu_custom_call" | custom-call | flops 805306368 | bytes 60000000 | tf_op jit(solution)/shard_map/partials/pallas_call | solution.py:186
  27.7 0.0 copy-done.3
  27.7 40.5 %exchange.1 = (bf16[1024,128]{1,0:T(8,128)(2,1)S(1)}, f32[32,1024]{1,0:T(8,128)S(1)}) custom-call(f32[8]{0:T(128)S(1)} %copy-done.3, bf16[16,528,128]{2,1,0:T(8,128)(2,1)S(1)} %bitcast.8), custom_call_target="tpu_custom_call" | custom-call | tf_op jit(solution)/shard_map/exchange/pallas_call | solution.py:324
  68.2 0.7 %copy.22 = bf16[1024,128]{1,0:T(8,128)(2,1)} copy(bf16[1024,128]{1,0:T(8,128)(2,1)S(1)} %get-tuple-element.6) | data formatting | bytes 524288
  68.9 0.7 copy.23
  (1 shorter events, 0.0 us)
Async XLA Ops:
  0.6 5.0 %copy-start.2 = (s32[2048,4]{0,1:T(4,128)S(1)}, s32[2048,4]{0,1:T(4,128)}, u32[]{:S(2)}) copy-start(s32[2048,4]{0,1:T(4,128)} %param.10) | copy-start | bytes 98308
  0.6 5.0 %copy-start.1 = (f32[2,4,2048]{2,1,0:T(4,128)S(1)}, f32[2,4,2048]{2,1,0:T(4,128)}, u32[]{:S(2)}) copy-start(f32[2,4,2048]{2,1,0:T(4,128)} %coef_ref.1) | copy-start | bytes 196612
  0.6 5.0 %copy-start = (bf16[2048,128]{1,0:T(8,128)(2,1)S(1)}, bf16[2048,128]{1,0:T(8,128)(2,1)}, u32[]{:S(2)}) copy-start(bf16[2048,128]{1,0:T(8,128)(2,1)} %field_ref.1) | copy-start | bytes 1572868
  12.6 15.1 %copy-start.3 = (f32[8]{0:T(128)S(1)}, f32[8]{0:T(128)}, u32[]{:S(2)}) copy-start(f32[8]{0:T(128)} %level_ref.1) | copy-start | bytes 100
